TPU v7x, 32 devices: a whole 2x2x4 slice. The times are simulated.
32 devices in a mesh: gx: 8 (over z, x), gy: 4 (over y, core).
Axes of the slice: x: 2, y: 2, z: 4, core: 2. Of those that a mesh axis runs over, the one named last changes fastest.
Arguments:
- forcing: float32 [3, 64, 64, 512], P(None, 'gx', 'gy'), may hold values from -6.5 to 6.5
- phase_ids: int32 [64, 64, 512], P('gx', 'gy'), may hold values from 0 to 3
Outputs:
- velocity: float32 [3, 64, 64, 512], P(None, 'gx', 'gy')
All inputs are finite; a program needn't handle non-finite values.
Results may differ from a plain program's by a relative error of at most 0.0003.
Values sent between devices are 32-bit elements; how exact they have to be, the bound alone decides.
A program may use at most 128 MiB of HBM per device.

v0:
```python
import jax
import jax.numpy as jnp
from jax import lax
from jax.sharding import PartitionSpec as P

COARSE_SWEEPS = 6


viscosities = (0.2, 0.6, 1.5, 4.0)
relax_weight = 2.0 / 3.0


def extended(array, sides, width):
    for axis, dim in sides:
        size, length = (lax.axis_size(axis), array.shape[dim])
        up = [(i, (i + 1) % size) for i in range(size - 1)]
        down = [(j, i) for i, j in up]
        last = lax.slice_in_dim(array, length - width, length, axis=dim)
        initial = lax.slice_in_dim(array, 0, width, axis=dim)
        before = lax.ppermute(last, axis, up)
        after = lax.ppermute(initial, axis, down)
        array = jnp.concatenate([before, array, after], axis=dim)
    return array


def lookup(phase_ids):
    viscosity = jnp.zeros(phase_ids.shape, jnp.float32)
    for material, visc_value in enumerate(viscosities):
        viscosity = viscosity + jnp.where(
            phase_ids == material, jnp.float32(visc_value), jnp.float32(0.0)
        )
    return viscosity


def restrict(values):
    extent = values.shape
    leading = extent[:-3]
    blocks = values.reshape(leading + (extent[-3] // 2, 2, extent[-2] // 2, 2, extent[-1] // 2, 2))
    return jnp.mean(blocks, axis=(-5, -3, -1))


def prolong(values):
    return jnp.repeat(jnp.repeat(jnp.repeat(values, 2, axis=-3), 2, axis=-2), 2, axis=-1)


def face_set(wide_visc, spacing):
    center = wide_visc[1:-1, 1:-1, :]
    z_padded = jnp.pad(center, ((0, 0), (0, 0), (1, 1)))
    besides = (
        wide_visc[2:, 1:-1, :],
        wide_visc[:-2, 1:-1, :],
        wide_visc[1:-1, 2:, :],
        wide_visc[1:-1, :-2, :],
        z_padded[:, :, 2:],
        z_padded[:, :, :-2],
    )
    coeffs = tuple(
        (jnp.where(beside > 0.0, 0.5 * (center + beside), center) / spacing for beside in besides)
    )
    diagonal = coeffs[0]
    for entry in coeffs[1:]:
        diagonal = diagonal + entry
    inside = center > 0.0
    inverse = jnp.where(inside, 1.0 / jnp.where(inside, diagonal, 1.0), 0.0)
    return (coeffs, inverse)


def crop_set(level_set):
    coeffs, inverse = level_set
    return (tuple((entry[1:-1, 1:-1, :] for entry in coeffs)), inverse[1:-1, 1:-1, :])


def apply_operator(wide_field, coeffs):
    center = wide_field[..., 1:-1, 1:-1, :]
    padding = [(0, 0)] * (center.ndim - 1) + [(1, 1)]
    z_padded = jnp.pad(center, padding)
    besides = (
        wide_field[..., 2:, 1:-1, :],
        wide_field[..., :-2, 1:-1, :],
        wide_field[..., 1:-1, 2:, :],
        wide_field[..., 1:-1, :-2, :],
        z_padded[..., 2:],
        z_padded[..., :-2],
    )
    summed = jnp.zeros_like(center)
    for face_coeff, beside in zip(coeffs, besides):
        summed = summed + face_coeff * (center - beside)
    return summed


def rim_field(current):
    return extended(current, (("gx", 1), ("gy", 2)), 1)


def deep_rim(current):
    return extended(current, (("gx", 1), ("gy", 2)), 2)


def jacobi_sweep(current, source, level_set):
    coeffs, inverse = level_set
    return current + relax_weight * (source - apply_operator(rim_field(current), coeffs)) * inverse


def per_device(forcing, phase_ids):
    viscosity = lookup(phase_ids)
    wide_sets = []
    for level_index in range(2):
        wide_visc = extended(viscosity, (("gx", 0), ("gy", 1)), 2)
        wide_sets.append(face_set(wide_visc, 4.0**level_index))
        viscosity = restrict(viscosity)
    narrow_sets = [crop_set(entry) for entry in wide_sets]

    def descend(source, level_index):
        coeffs, inverse = narrow_sets[level_index]
        current = relax_weight * source * inverse
        stacked = deep_rim(jnp.concatenate((current, source), axis=0))
        wide_coeffs, wide_inverse = wide_sets[level_index]
        wide_source = stacked[3:, 1:-1, 1:-1, :]
        middle = (
            stacked[:3, 1:-1, 1:-1, :]
            + relax_weight * (wide_source - apply_operator(stacked[:3], wide_coeffs)) * wide_inverse
        )
        current = middle[:, 1:-1, 1:-1, :]
        residual = source - apply_operator(middle, coeffs)
        return (current, restrict(residual), wide_source)

    def ascend(current, source, wide_source, level_index):
        wide_field = deep_rim(current)
        wide_coeffs, wide_inverse = wide_sets[level_index]
        middle = (
            wide_field[:, 1:-1, 1:-1, :]
            + relax_weight * (wide_source - apply_operator(wide_field, wide_coeffs)) * wide_inverse
        )
        coeffs, inverse = narrow_sets[level_index]
        return (
            middle[:, 1:-1, 1:-1, :]
            + relax_weight * (source - apply_operator(middle, coeffs)) * inverse
        )

    fine_velocity, source_one, wide_zero = descend(forcing, 0)
    middle_velocity, source_two, wide_one = descend(source_one, 1)
    wide_visc = extended(viscosity, (("gx", 0), ("gy", 1)), 1)
    coarse_set = face_set(wide_visc, 16.0)
    coarse = relax_weight * source_two * coarse_set[1]
    for repeat in range(COARSE_SWEEPS - 1):
        coarse = jacobi_sweep(coarse, source_two, coarse_set)
    middle_velocity = ascend(middle_velocity + prolong(coarse), source_one, wide_one, 1)
    fine_velocity = ascend(fine_velocity + prolong(middle_velocity), forcing, wide_zero, 0)
    return fine_velocity


def solution(mesh):
    return jax.shard_map(
        per_device,
        mesh=mesh,
        in_specs=(P(None, "gx", "gy", None), P("gx", "gy", None)),
        out_specs=P(None, "gx", "gy", None),
        check_vma=False,
    )
```

profile of v0, /device:TPU:17, one launch (start us, length us, event | category | flops | bytes accessed | tf_op | source)
XLA Modules:
  0.0 348.6 jit_solution(3945252990801707345)
XLA Ops:
  1.1 3.0 collective-permute-start.1
  4.1 2.3 collective-permute-start
  6.4 18.1 %reshape.67 = f32[4,2,8,2,256,2]{5,4,3,2,1,0:T(8,128)} reshape(f32[8,16,512]{2,1,0:T(8,128)S(1)} %select_add_fusion) | data formatting | bytes 524288 | tf_op jit(solution)/shard_map/reshape | solution.py:38
  24.5 7.0 %reduce_sum.37 = f32[4,8,256]{2,1,0:T(8,128)S(1)} reduce(f32[4,2,8,2,256,2]{5,4,3,2,1,0:T(8,128)} %reshape.67, f32[]{:T(128)} %constant.21.clone.1), dimensions={1,3,5}, to_apply=%region_1.2 | reduce | flops 57344 | bytes 294916 | tf_op jit(solution)/shard_map/reduce_sum | solution.py:39
  31.5 3.9 %collective-permute-start.9 = (f32[2,8,256]{2,1,0:T(8,128)S(1)}, f32[2,8,256]{2,1,0:T(8,128)S(1)}, u32[]{:S(2)}, u32[]{:S(2)}) collective-permute-start(f32[2,8,256]{2,1,0:T(8,128)S(1)} %get-tuple-element.52), channel_id=1, source_target_pairs={{4,0},{8,4},{12,8},{16,12},{20,16},{24,20},{28,24},{5,1},{9,5},{13... | collective-permute-start | bytes 49160 | tf_op jit(solution)/shard_map/ppermute | solution.py:21
  39.8 3.4 collective-permute-start.3
  43.3 3.0 collective-permute-start.2
  49.7 4.4 %collective-permute-start.5 = (f32[6,2,16,512]{3,2,1,0:T(8,128)S(1)}, f32[6,2,16,512]{3,2,1,0:T(8,128)S(1)}, u32[]{:S(2)}, u32[]{:S(2)}) collective-permute-start(f32[6,2,16,512]{3,2,1,0:T(8,128)S(1)} %get-tuple-element.22), channel_id=1, source_target_pairs={{4,0},{8,4},{12,8},{16,12},{20,16},{24,20},{28,24},{5,1},{9,5},{13... | collective-permute-start | bytes 1179656 | tf_op jit(solution)/shard_map/ppermute | solution.py:21
  56.2 4.3 %collective-permute-start.17 = (f32[1,4,128]{2,1,0:T(4,128)S(1)}, f32[1,4,128]{2,1,0:T(4,128)S(1)}, u32[]{:S(2)}, u32[]{:S(2)}) collective-permute-start(f32[1,4,128]{2,1,0:T(4,128)S(1)} %get-tuple-element.80), channel_id=1, source_target_pairs={{0,4},{4,8},{8,12},{12,16},{16,20},{20,24},{24,28},{1,5},{5,9},{9,... | collective-permute-start | bytes 6152 | tf_op jit(solution)/shard_map/ppermute | solution.py:20
  64.4 7.8 %collective-permute-done.17 = f32[1,4,128]{2,1,0:T(4,128)S(1)} collective-permute-done((f32[1,4,128]{2,1,0:T(4,128)S(1)}, f32[1,4,128]{2,1,0:T(4,128)S(1)}, u32[]{:S(2)}, u32[]{:S(2)}) %collective-permute-start.17) | collective-permute-done | bytes 2080 | tf_op jit(solution)/shard_map/ppermute | solution.py:20
  72.2 2.8 collective-permute-start.10
  77.5 3.6 %collective-permute-start.19 = (f32[4,1,128]{2,1,0:T(1,128)S(1)}, f32[4,1,128]{2,1,0:T(1,128)}, u32[]{:S(2)}, u32[]{:S(2)}) collective-permute-start(f32[4,1,128]{2,1,0:T(1,128)S(1)} %get-tuple-element.73), channel_id=1, source_target_pairs={{0,1},{1,2},{2,3},{4,5},{5,6},{6,7},{8,9},{9,10},{10,11},{12,13},{... | collective-permute-start | bytes 6152 | tf_op jit(solution)/shard_map/ppermute | solution.py:20
  83.5 3.8 %collective-permute-start.6 = (f32[6,12,2,512]{3,2,1,0:T(2,128)S(1)}, f32[6,12,2,512]{3,2,1,0:T(2,128)S(1)}, u32[]{:S(2)}, u32[]{:S(2)}) collective-permute-start(f32[6,12,2,512]{3,2,1,0:T(2,128)S(1)} %get-tuple-element.19), channel_id=1, source_target_pairs={{0,1},{1,2},{2,3},{4,5},{5,6},{6,7},{8,9},{9,10},{10,11},{12,13},{... | collective-permute-start | bytes 884744 | tf_op jit(solution)/shard_map/ppermute | solution.py:20
  91.8 3.0 fusion.6
  95.9 51.6 %reshape.66 = f32[3,4,2,8,2,256,2]{6,5,4,3,2,1,0:T(8,128)} reshape(f32[3,8,16,512]{3,2,1,0:T(8,128)S(1)} %fusion.40) | data formatting | bytes 1572864 | tf_op jit(solution)/shard_map/reshape | solution.py:38
  147.5 17.8 %reduce_sum.36 = f32[3,4,8,256]{3,2,1,0:T(8,128)S(1)} reduce(f32[3,4,2,8,2,256,2]{6,5,4,3,2,1,0:T(8,128)} %reshape.66, f32[]{:T(128)} %constant.21.clone.1), dimensions={2,4,6}, to_apply=%region_0.1 | reduce | flops 172032 | bytes 884740 | tf_op jit(solution)/shard_map/reduce_sum | solution.py:39
  165.4 4.1 %collective-permute-start.13 = (f32[6,2,8,256]{3,2,1,0:T(8,128)S(1)}, f32[6,2,8,256]{3,2,1,0:T(8,128)S(1)}, u32[]{:S(2)}, u32[]{:S(2)}) collective-permute-start(f32[6,2,8,256]{3,2,1,0:T(8,128)S(1)} %get-tuple-element.40), channel_id=1, source_target_pairs={{4,0},{8,4},{12,8},{16,12},{20,16},{24,20},{28,24},{5,1},{9,5},{13... | collective-permute-start | bytes 294920 | tf_op jit(solution)/shard_map/ppermute | solution.py:21
  177.8 6.0 %collective-permute-start.14 = (f32[6,8,2,256]{3,1,2,0:T(8,128)S(1)}, f32[6,8,2,256]{3,1,2,0:T(8,128)S(1)}, u32[]{:S(2)}, u32[]{:S(2)}) collective-permute-start(f32[6,8,2,256]{3,1,2,0:T(8,128)S(1)} %copy.205), channel_id=1, source_target_pairs={{0,1},{1,2},{2,3},{4,5},{5,6},{6,7},{8,9},{9,10},{10,11},{12,13},{... | collective-permute-start | bytes 294920 | tf_op jit(solution)/shard_map/ppermute | solution.py:20
  186.9 8.4 %reshape.68 = f32[3,2,2,4,2,128,2]{6,5,4,3,2,1,0:T(8,128)} reshape(f32[3,4,8,256]{3,2,1,0:T(8,128)} %fusion.106) | data formatting | bytes 196608 | tf_op jit(solution)/shard_map/reshape | solution.py:38
  195.2 3.3 reduce_sum.38
  201.1 3.4 collective-permute-start.21
  206.4 5.5 %collective-permute-start.23 = (f32[3,4,1,128]{3,2,1,0:T(1,128)S(1)}, f32[3,4,1,128]{3,2,1,0:T(1,128)S(1)}, u32[]{:S(2)}, u32[]{:S(2)}) collective-permute-start(f32[3,4,1,128]{3,2,1,0:T(1,128)S(1)} %get-tuple-element.62), channel_id=1, source_target_pairs={{0,1},{1,2},{2,3},{4,5},{5,6},{6,7},{8,9},{9,10},{10,11},{12,13},{... | collective-permute-start | bytes 18440 | tf_op jit(solution)/shard_map/ppermute | solution.py:20
  217.6 2.6 collective-permute-start.24
  220.3 2.7 collective-permute-start.25
  222.9 2.6 collective-permute-done.25
  225.6 3.4 collective-permute-start.27
  230.9 3.0 collective-permute-done.26
  236.6 3.4 collective-permute-start.29
  241.9 3.1 collective-permute-start.31
  246.9 3.0 collective-permute-done.30
  252.7 3.4 collective-permute-start.33
  258.0 3.1 collective-permute-start.35
  263.0 3.0 collective-permute-done.34
  268.7 3.4 collective-permute-start.37
  274.0 3.1 collective-permute-start.39
  279.1 3.0 collective-permute-done.38
  285.5 2.8 broadcast_in_dim.48
  288.3 2.5 copy.195
  293.7 3.4 collective-permute-start.40
  297.1 2.4 collective-permute-done.40
  301.5 3.9 %collective-permute-start.42 = (f32[3,8,2,256]{3,1,2,0:T(8,128)S(1)}, f32[3,8,2,256]{3,1,2,0:T(8,128)S(1)}, u32[]{:S(2)}, u32[]{:S(2)}) collective-permute-start(f32[3,8,2,256]{3,1,2,0:T(8,128)S(1)} %copy.207), channel_id=1, source_target_pairs={{0,1},{1,2},{2,3},{4,5},{5,6},{6,7},{8,9},{9,10},{10,11},{12,13},{... | collective-permute-start | bytes 147464 | tf_op jit(solution)/shard_map/ppermute | solution.py:20
  307.8 2.3 copy.203
  310.1 4.9 %broadcast_in_dim.51 = f32[3,8,16,256,2]{2,1,4,3,0:T(8,128)} broadcast(f32[3,8,16,256]{2,1,3,0:T(8,128)} %copy.203), dimensions={0,1,2,3} | broadcast | bytes 1179648 | tf_op jit(solution)/shard_map/broadcast_in_dim | solution.py:43
  314.9 4.3 %copy.204 = f32[3,8,16,512]{3,2,1,0:T(8,128)S(1)} copy(f32[3,8,16,512]{2,1,3,0:T(8,128)} %bitcast.14) | data formatting | bytes 1572864 | tf_op jit(solution)/shard_map/reshape | solution.py:43
  321.5 3.4 collective-permute-start.44
  324.8 6.4 %collective-permute-done.45 = f32[3,2,16,512]{3,2,1,0:T(8,128)S(1)} collective-permute-done((f32[3,2,16,512]{3,2,1,0:T(8,128)S(1)}, f32[3,2,16,512]{3,2,1,0:T(8,128)S(1)}, u32[]{:S(2)}, u32[]{:S(2)}) %collective-permute-start.45) | collective-permute-done | bytes 196640 | tf_op jit(solution)/shard_map/ppermute | solution.py:21
  333.4 3.8 %collective-permute-start.46 = (f32[3,12,2,512]{3,2,1,0:T(2,128)S(1)}, f32[3,12,2,512]{3,2,1,0:T(2,128)S(1)}, u32[]{:S(2)}, u32[]{:S(2)}) collective-permute-start(f32[3,12,2,512]{3,2,1,0:T(2,128)S(1)} %get-tuple-element.23), channel_id=1, source_target_pairs={{0,1},{1,2},{2,3},{4,5},{5,6},{6,7},{8,9},{9,10},{10,11},{12,13},{... | collective-permute-start | bytes 442376 | tf_op jit(solution)/shard_map/ppermute | solution.py:20
  341.4 4.0 %fusion.15 = f32[3,10,18,512]{3,2,1,0:T(8,128)S(1)} fusion(f32[3,10,18,512]{3,2,1,0:T(8,128)S(1)} %slice.804, f32[3,12,2,512]{3,2,1,0:T(2,128)S(1)} %collective-permute-done.46, f32[3,2,16,512]{3,2,1,0:T(8,128)S(1)} %collective-permute-done.45, f32[3,8,16,512]{3,2,1,0:T(8,128)S(1)} %slice_add_fusion.1, f32[3,2,16,512]{3,2,1,0:T(8,128)S(1)} %collective-permute-done.44, ...), kind=kLoop, calls=%fused_computation.21 | loop fusion | flops 7188480 | bytes 9584640 | tf_op jit(solution)/shard_map/add | solution.py:131
  (282 shorter events, 89.7 us)
Async XLA Ops:
  1.1 38.7 %collective-permute-start.1 = (f32[2,16,512]{2,1,0:T(8,128)S(1)}, f32[2,16,512]{2,1,0:T(8,128)S(1)}, u32[]{:S(2)}, u32[]{:S(2)}) collective-permute-start(f32[2,16,512]{2,1,0:T(8,128)S(1)} %get-tuple-element.36), channel_id=1, source_target_pairs={{4,0},{8,4},{12,8},{16,12},{20,16},{24,20},{28,24},{5,1},{9,5},{13... | collective-permute-start | bytes 196616 | tf_op jit(solution)/shard_map/ppermute | solution.py:21
  4.1 35.7 %collective-permute-start = (f32[2,16,512]{2,1,0:T(8,128)S(1)}, f32[2,16,512]{2,1,0:T(8,128)S(1)}, u32[]{:S(2)}, u32[]{:S(2)}) collective-permute-start(f32[2,16,512]{2,1,0:T(8,128)S(1)} %get-tuple-element.35), channel_id=1, source_target_pairs={{0,4},{4,8},{8,12},{12,16},{16,20},{20,24},{24,28},{1,5},{5,9},{9,... | collective-permute-start | bytes 196616 | tf_op jit(solution)/shard_map/ppermute | solution.py:20
  31.5 29.0 %collective-permute-start.9 = (f32[2,8,256]{2,1,0:T(8,128)S(1)}, f32[2,8,256]{2,1,0:T(8,128)S(1)}, u32[]{:S(2)}, u32[]{:S(2)}) collective-permute-start(f32[2,8,256]{2,1,0:T(8,128)S(1)} %get-tuple-element.52), channel_id=1, source_target_pairs={{4,0},{8,4},{12,8},{16,12},{20,16},{24,20},{28,24},{5,1},{9,5},{13... | collective-permute-start | bytes 49160 | tf_op jit(solution)/shard_map/ppermute | solution.py:21
  35.4 27.0 %collective-permute-start.8 = (f32[2,8,256]{2,1,0:T(8,128)S(1)}, f32[2,8,256]{2,1,0:T(8,128)S(1)}, u32[]{:S(2)}, u32[]{:S(2)}) collective-permute-start(f32[2,8,256]{2,1,0:T(8,128)S(1)} %get-tuple-element.51), channel_id=1, source_target_pairs={{0,4},{4,8},{8,12},{12,16},{16,20},{20,24},{24,28},{1,5},{5,9},{9,... | collective-permute-start | bytes 49160 | tf_op jit(solution)/shard_map/ppermute | solution.py:20
  39.8 6.5 %collective-permute-start.3 = (f32[12,2,512]{2,1,0:T(2,128)S(1)}, f32[12,2,512]{2,1,0:T(2,128)S(1)}, u32[]{:S(2)}, u32[]{:S(2)}) collective-permute-start(f32[12,2,512]{2,1,0:T(2,128)S(1)} %get-tuple-element.34), channel_id=1, source_target_pairs={{1,0},{2,1},{3,2},{5,4},{6,5},{7,6},{9,8},{10,9},{11,10},{13,12},{... | collective-permute-start | bytes 147464 | tf_op jit(solution)/shard_map/ppermute | solution.py:21
  43.3 4.2 %collective-permute-start.2 = (f32[12,2,512]{2,1,0:T(2,128)S(1)}, f32[12,2,512]{2,1,0:T(2,128)S(1)}, u32[]{:S(2)}, u32[]{:S(2)}) collective-permute-start(f32[12,2,512]{2,1,0:T(2,128)S(1)} %get-tuple-element.33), channel_id=1, source_target_pairs={{0,1},{1,2},{2,3},{4,5},{5,6},{6,7},{8,9},{9,10},{10,11},{12,13},{... | collective-permute-start | bytes 147464 | tf_op jit(solution)/shard_map/ppermute | solution.py:20
  49.7 31.5 %collective-permute-start.5 = (f32[6,2,16,512]{3,2,1,0:T(8,128)S(1)}, f32[6,2,16,512]{3,2,1,0:T(8,128)S(1)}, u32[]{:S(2)}, u32[]{:S(2)}) collective-permute-start(f32[6,2,16,512]{3,2,1,0:T(8,128)S(1)} %get-tuple-element.22), channel_id=1, source_target_pairs={{4,0},{8,4},{12,8},{16,12},{20,16},{24,20},{28,24},{5,1},{9,5},{13... | collective-permute-start | bytes 1179656 | tf_op jit(solution)/shard_map/ppermute | solution.py:21
  54.2 27.1 %collective-permute-start.4 = (f32[6,2,16,512]{3,2,1,0:T(8,128)S(1)}, f32[6,2,16,512]{3,2,1,0:T(8,128)S(1)}, u32[]{:S(2)}, u32[]{:S(2)}) collective-permute-start(f32[6,2,16,512]{3,2,1,0:T(8,128)S(1)} %get-tuple-element.21), channel_id=1, source_target_pairs={{0,4},{4,8},{8,12},{12,16},{16,20},{20,24},{24,28},{1,5},{5,9},{9,... | collective-permute-start | bytes 1179656 | tf_op jit(solution)/shard_map/ppermute | solution.py:20
  56.2 15.9 %collective-permute-start.17 = (f32[1,4,128]{2,1,0:T(4,128)S(1)}, f32[1,4,128]{2,1,0:T(4,128)S(1)}, u32[]{:S(2)}, u32[]{:S(2)}) collective-permute-start(f32[1,4,128]{2,1,0:T(4,128)S(1)} %get-tuple-element.80), channel_id=1, source_target_pairs={{0,4},{4,8},{8,12},{12,16},{16,20},{20,24},{24,28},{1,5},{5,9},{9,... | collective-permute-start | bytes 6152 | tf_op jit(solution)/shard_map/ppermute | solution.py:20
  60.5 14.5 %collective-permute-start.16 = (f32[1,4,128]{2,1,0:T(4,128)S(1)}, f32[1,4,128]{2,1,0:T(4,128)S(1)}, u32[]{:S(2)}, u32[]{:S(2)}) collective-permute-start(f32[1,4,128]{2,1,0:T(4,128)S(1)} %get-tuple-element.79), channel_id=1, source_target_pairs={{4,0},{8,4},{12,8},{16,12},{20,16},{24,20},{28,24},{5,1},{9,5},{13... | collective-permute-start | bytes 6152 | tf_op jit(solution)/shard_map/ppermute | solution.py:21
  62.5 15.0 %collective-permute-start.11 = (f32[8,2,256]{2,1,0:T(2,128)S(1)}, f32[8,2,256]{2,1,0:T(2,128)S(1)}, u32[]{:S(2)}, u32[]{:S(2)}) collective-permute-start(f32[8,2,256]{2,1,0:T(2,128)S(1)} %get-tuple-element.50), channel_id=1, source_target_pairs={{1,0},{2,1},{3,2},{5,4},{6,5},{7,6},{9,8},{10,9},{11,10},{13,12},{... | collective-permute-start | bytes 49160 | tf_op jit(solution)/shard_map/ppermute | solution.py:21
  72.2 9.0 %collective-permute-start.10 = (f32[8,2,256]{2,1,0:T(2,128)S(1)}, f32[8,2,256]{2,1,0:T(2,128)S(1)}, u32[]{:S(2)}, u32[]{:S(2)}) collective-permute-start(f32[8,2,256]{2,1,0:T(2,128)S(1)} %get-tuple-element.49), channel_id=1, source_target_pairs={{0,1},{1,2},{2,3},{4,5},{5,6},{6,7},{8,9},{9,10},{10,11},{12,13},{... | collective-permute-start | bytes 49160 | tf_op jit(solution)/shard_map/ppermute | solution.py:20
  75.6 96.0 %collective-permute-start.18 = (f32[4,1,128]{2,1,0:T(1,128)}, f32[4,1,128]{2,1,0:T(1,128)S(1)}, u32[]{:S(2)}, u32[]{:S(2)}) collective-permute-start(f32[4,1,128]{2,1,0:T(1,128)} %get-tuple-element.74), channel_id=1, source_target_pairs={{1,0},{2,1},{3,2},{5,4},{6,5},{7,6},{9,8},{10,9},{11,10},{13,12},{... | collective-permute-start | bytes 6152 | tf_op jit(solution)/shard_map/ppermute | solution.py:21
  77.5 94.7 %collective-permute-start.19 = (f32[4,1,128]{2,1,0:T(1,128)S(1)}, f32[4,1,128]{2,1,0:T(1,128)}, u32[]{:S(2)}, u32[]{:S(2)}) collective-permute-start(f32[4,1,128]{2,1,0:T(1,128)S(1)} %get-tuple-element.73), channel_id=1, source_target_pairs={{0,1},{1,2},{2,3},{4,5},{5,6},{6,7},{8,9},{9,10},{10,11},{12,13},{... | collective-permute-start | bytes 6152 | tf_op jit(solution)/shard_map/ppermute | solution.py:20
  81.5 8.0 %collective-permute-start.7 = (f32[6,12,2,512]{3,2,1,0:T(2,128)S(1)}, f32[6,12,2,512]{3,2,1,0:T(2,128)S(1)}, u32[]{:S(2)}, u32[]{:S(2)}) collective-permute-start(f32[6,12,2,512]{3,2,1,0:T(2,128)S(1)} %get-tuple-element.20), channel_id=1, source_target_pairs={{1,0},{2,1},{3,2},{5,4},{6,5},{7,6},{9,8},{10,9},{11,10},{13,12},{... | collective-permute-start | bytes 884744 | tf_op jit(solution)/shard_map/ppermute | solution.py:21
  83.5 7.3 %collective-permute-start.6 = (f32[6,12,2,512]{3,2,1,0:T(2,128)S(1)}, f32[6,12,2,512]{3,2,1,0:T(2,128)S(1)}, u32[]{:S(2)}, u32[]{:S(2)}) collective-permute-start(f32[6,12,2,512]{3,2,1,0:T(2,128)S(1)} %get-tuple-element.19), channel_id=1, source_target_pairs={{0,1},{1,2},{2,3},{4,5},{5,6},{6,7},{8,9},{9,10},{10,11},{12,13},{... | collective-permute-start | bytes 884744 | tf_op jit(solution)/shard_map/ppermute | solution.py:20
  165.4 8.1 %collective-permute-start.13 = (f32[6,2,8,256]{3,2,1,0:T(8,128)S(1)}, f32[6,2,8,256]{3,2,1,0:T(8,128)S(1)}, u32[]{:S(2)}, u32[]{:S(2)}) collective-permute-start(f32[6,2,8,256]{3,2,1,0:T(8,128)S(1)} %get-tuple-element.40), channel_id=1, source_target_pairs={{4,0},{8,4},{12,8},{16,12},{20,16},{24,20},{28,24},{5,1},{9,5},{13... | collective-permute-start | bytes 294920 | tf_op jit(solution)/shard_map/ppermute | solution.py:21
  169.5 6.3 %collective-permute-start.12 = (f32[6,2,8,256]{3,2,1,0:T(8,128)S(1)}, f32[6,2,8,256]{3,2,1,0:T(8,128)S(1)}, u32[]{:S(2)}, u32[]{:S(2)}) collective-permute-start(f32[6,2,8,256]{3,2,1,0:T(8,128)S(1)} %get-tuple-element.39), channel_id=1, source_target_pairs={{0,4},{4,8},{8,12},{12,16},{16,20},{20,24},{24,28},{1,5},{5,9},{9,... | collective-permute-start | bytes 294920 | tf_op jit(solution)/shard_map/ppermute | solution.py:20
  175.9 8.7 %collective-permute-start.15 = (f32[6,8,2,256]{3,1,2,0:T(8,128)S(1)}, f32[6,8,2,256]{3,1,2,0:T(8,128)S(1)}, u32[]{:S(2)}, u32[]{:S(2)}) collective-permute-start(f32[6,8,2,256]{3,1,2,0:T(8,128)S(1)} %copy.206), channel_id=1, source_target_pairs={{1,0},{2,1},{3,2},{5,4},{6,5},{7,6},{9,8},{10,9},{11,10},{13,12},{... | collective-permute-start | bytes 294920 | tf_op jit(solution)/shard_map/ppermute | solution.py:21
  177.8 7.6 %collective-permute-start.14 = (f32[6,8,2,256]{3,1,2,0:T(8,128)S(1)}, f32[6,8,2,256]{3,1,2,0:T(8,128)S(1)}, u32[]{:S(2)}, u32[]{:S(2)}) collective-permute-start(f32[6,8,2,256]{3,1,2,0:T(8,128)S(1)} %copy.205), channel_id=1, source_target_pairs={{0,1},{1,2},{2,3},{4,5},{5,6},{6,7},{8,9},{9,10},{10,11},{12,13},{... | collective-permute-start | bytes 294920 | tf_op jit(solution)/shard_map/ppermute | solution.py:20
  199.2 5.3 %collective-permute-start.20 = (f32[3,1,4,128]{3,2,1,0:T(4,128)S(1)}, f32[3,1,4,128]{3,2,1,0:T(4,128)S(1)}, u32[]{:S(2)}, u32[]{:S(2)}) collective-permute-start(f32[3,1,4,128]{3,2,1,0:T(4,128)S(1)} %get-tuple-element.72), channel_id=1, source_target_pairs={{4,0},{8,4},{12,8},{16,12},{20,16},{24,20},{28,24},{5,1},{9,5},{13... | collective-permute-start | bytes 18440 | tf_op jit(solution)/shard_map/ppermute | solution.py:21
  201.1 5.3 %collective-permute-start.21 = (f32[3,1,4,128]{3,2,1,0:T(4,128)S(1)}, f32[3,1,4,128]{3,2,1,0:T(4,128)S(1)}, u32[]{:S(2)}, u32[]{:S(2)}) collective-permute-start(f32[3,1,4,128]{3,2,1,0:T(4,128)S(1)} %get-tuple-element.71), channel_id=1, source_target_pairs={{0,4},{4,8},{8,12},{12,16},{16,20},{20,24},{24,28},{1,5},{5,9},{9,... | collective-permute-start | bytes 18440 | tf_op jit(solution)/shard_map/ppermute | solution.py:20
  206.4 8.3 %collective-permute-start.23 = (f32[3,4,1,128]{3,2,1,0:T(1,128)S(1)}, f32[3,4,1,128]{3,2,1,0:T(1,128)S(1)}, u32[]{:S(2)}, u32[]{:S(2)}) collective-permute-start(f32[3,4,1,128]{3,2,1,0:T(1,128)S(1)} %get-tuple-element.62), channel_id=1, source_target_pairs={{0,1},{1,2},{2,3},{4,5},{5,6},{6,7},{8,9},{9,10},{10,11},{12,13},{... | collective-permute-start | bytes 18440 | tf_op jit(solution)/shard_map/ppermute | solution.py:20
  211.9 4.9 %collective-permute-start.22 = (f32[3,4,1,128]{3,2,1,0:T(1,128)S(1)}, f32[3,4,1,128]{3,2,1,0:T(1,128)S(1)}, u32[]{:S(2)}, u32[]{:S(2)}) collective-permute-start(f32[3,4,1,128]{3,2,1,0:T(1,128)S(1)} %get-tuple-element.61), channel_id=1, source_target_pairs={{1,0},{2,1},{3,2},{5,4},{6,5},{7,6},{9,8},{10,9},{11,10},{13,12},{... | collective-permute-start | bytes 18440 | tf_op jit(solution)/shard_map/ppermute | solution.py:21
  217.6 5.3 %collective-permute-start.24 = (f32[3,1,4,128]{3,2,1,0:T(4,128)S(1)}, f32[3,1,4,128]{3,2,1,0:T(4,128)S(1)}, u32[]{:S(2)}, u32[]{:S(2)}) collective-permute-start(f32[3,1,4,128]{3,2,1,0:T(4,128)S(1)} %get-tuple-element.70), channel_id=1, source_target_pairs={{4,0},{8,4},{12,8},{16,12},{20,16},{24,20},{28,24},{5,1},{9,5},{13... | collective-permute-start | bytes 18440 | tf_op jit(solution)/shard_map/ppermute | solution.py:21
  220.3 5.3 %collective-permute-start.25 = (f32[3,1,4,128]{3,2,1,0:T(4,128)S(1)}, f32[3,1,4,128]{3,2,1,0:T(4,128)S(1)}, u32[]{:S(2)}, u32[]{:S(2)}) collective-permute-start(f32[3,1,4,128]{3,2,1,0:T(4,128)S(1)} %get-tuple-element.69), channel_id=1, source_target_pairs={{0,4},{4,8},{8,12},{12,16},{16,20},{20,24},{24,28},{1,5},{5,9},{9,... | collective-permute-start | bytes 18440 | tf_op jit(solution)/shard_map/ppermute | solution.py:20
  225.6 5.3 %collective-permute-start.27 = (f32[3,4,1,128]{3,2,1,0:T(1,128)S(1)}, f32[3,4,1,128]{3,2,1,0:T(1,128)S(1)}, u32[]{:S(2)}, u32[]{:S(2)}) collective-permute-start(f32[3,4,1,128]{3,2,1,0:T(1,128)S(1)} %get-tuple-element.60), channel_id=1, source_target_pairs={{0,1},{1,2},{2,3},{4,5},{5,6},{6,7},{8,9},{9,10},{10,11},{12,13},{... | collective-permute-start | bytes 18440 | tf_op jit(solution)/shard_map/ppermute | solution.py:20
  228.9 4.9 %collective-permute-start.26 = (f32[3,4,1,128]{3,2,1,0:T(1,128)S(1)}, f32[3,4,1,128]{3,2,1,0:T(1,128)S(1)}, u32[]{:S(2)}, u32[]{:S(2)}) collective-permute-start(f32[3,4,1,128]{3,2,1,0:T(1,128)S(1)} %get-tuple-element.59), channel_id=1, source_target_pairs={{1,0},{2,1},{3,2},{5,4},{6,5},{7,6},{9,8},{10,9},{11,10},{13,12},{... | collective-permute-start | bytes 18440 | tf_op jit(solution)/shard_map/ppermute | solution.py:21
  234.7 5.3 %collective-permute-start.28 = (f32[3,1,4,128]{3,2,1,0:T(4,128)S(1)}, f32[3,1,4,128]{3,2,1,0:T(4,128)S(1)}, u32[]{:S(2)}, u32[]{:S(2)}) collective-permute-start(f32[3,1,4,128]{3,2,1,0:T(4,128)S(1)} %get-tuple-element.68), channel_id=1, source_target_pairs={{4,0},{8,4},{12,8},{16,12},{20,16},{24,20},{28,24},{5,1},{9,5},{13... | collective-permute-start | bytes 18440 | tf_op jit(solution)/shard_map/ppermute | solution.py:21
  236.6 5.3 %collective-permute-start.29 = (f32[3,1,4,128]{3,2,1,0:T(4,128)S(1)}, f32[3,1,4,128]{3,2,1,0:T(4,128)S(1)}, u32[]{:S(2)}, u32[]{:S(2)}) collective-permute-start(f32[3,1,4,128]{3,2,1,0:T(4,128)S(1)} %get-tuple-element.67), channel_id=1, source_target_pairs={{0,4},{4,8},{8,12},{12,16},{16,20},{20,24},{24,28},{1,5},{5,9},{9,... | collective-permute-start | bytes 18440 | tf_op jit(solution)/shard_map/ppermute | solution.py:20
  241.9 5.0 %collective-permute-start.31 = (f32[3,4,1,128]{3,2,1,0:T(1,128)S(1)}, f32[3,4,1,128]{3,2,1,0:T(1,128)S(1)}, u32[]{:S(2)}, u32[]{:S(2)}) collective-permute-start(f32[3,4,1,128]{3,2,1,0:T(1,128)S(1)} %get-tuple-element.58), channel_id=1, source_target_pairs={{0,1},{1,2},{2,3},{4,5},{5,6},{6,7},{8,9},{9,10},{10,11},{12,13},{... | collective-permute-start | bytes 18440 | tf_op jit(solution)/shard_map/ppermute | solution.py:20
  245.0 4.9 %collective-permute-start.30 = (f32[3,4,1,128]{3,2,1,0:T(1,128)S(1)}, f32[3,4,1,128]{3,2,1,0:T(1,128)S(1)}, u32[]{:S(2)}, u32[]{:S(2)}) collective-permute-start(f32[3,4,1,128]{3,2,1,0:T(1,128)S(1)} %get-tuple-element.57), channel_id=1, source_target_pairs={{1,0},{2,1},{3,2},{5,4},{6,5},{7,6},{9,8},{10,9},{11,10},{13,12},{... | collective-permute-start | bytes 18440 | tf_op jit(solution)/shard_map/ppermute | solution.py:21
  250.7 5.3 %collective-permute-start.32 = (f32[3,1,4,128]{3,2,1,0:T(4,128)S(1)}, f32[3,1,4,128]{3,2,1,0:T(4,128)S(1)}, u32[]{:S(2)}, u32[]{:S(2)}) collective-permute-start(f32[3,1,4,128]{3,2,1,0:T(4,128)S(1)} %get-tuple-element.66), channel_id=1, source_target_pairs={{4,0},{8,4},{12,8},{16,12},{20,16},{24,20},{28,24},{5,1},{9,5},{13... | collective-permute-start | bytes 18440 | tf_op jit(solution)/shard_map/ppermute | solution.py:21
  252.7 5.3 %collective-permute-start.33 = (f32[3,1,4,128]{3,2,1,0:T(4,128)S(1)}, f32[3,1,4,128]{3,2,1,0:T(4,128)S(1)}, u32[]{:S(2)}, u32[]{:S(2)}) collective-permute-start(f32[3,1,4,128]{3,2,1,0:T(4,128)S(1)} %get-tuple-element.65), channel_id=1, source_target_pairs={{0,4},{4,8},{8,12},{12,16},{16,20},{20,24},{24,28},{1,5},{5,9},{9,... | collective-permute-start | bytes 18440 | tf_op jit(solution)/shard_map/ppermute | solution.py:20
  258.0 5.0 %collective-permute-start.35 = (f32[3,4,1,128]{3,2,1,0:T(1,128)S(1)}, f32[3,4,1,128]{3,2,1,0:T(1,128)S(1)}, u32[]{:S(2)}, u32[]{:S(2)}) collective-permute-start(f32[3,4,1,128]{3,2,1,0:T(1,128)S(1)} %get-tuple-element.56), channel_id=1, source_target_pairs={{0,1},{1,2},{2,3},{4,5},{5,6},{6,7},{8,9},{9,10},{10,11},{12,13},{... | collective-permute-start | bytes 18440 | tf_op jit(solution)/shard_map/ppermute | solution.py:20
  261.1 4.9 %collective-permute-start.34 = (f32[3,4,1,128]{3,2,1,0:T(1,128)S(1)}, f32[3,4,1,128]{3,2,1,0:T(1,128)S(1)}, u32[]{:S(2)}, u32[]{:S(2)}) collective-permute-start(f32[3,4,1,128]{3,2,1,0:T(1,128)S(1)} %get-tuple-element.55), channel_id=1, source_target_pairs={{1,0},{2,1},{3,2},{5,4},{6,5},{7,6},{9,8},{10,9},{11,10},{13,12},{... | collective-permute-start | bytes 18440 | tf_op jit(solution)/shard_map/ppermute | solution.py:21
  266.8 5.3 %collective-permute-start.36 = (f32[3,1,4,128]{3,2,1,0:T(4,128)S(1)}, f32[3,1,4,128]{3,2,1,0:T(4,128)S(1)}, u32[]{:S(2)}, u32[]{:S(2)}) collective-permute-start(f32[3,1,4,128]{3,2,1,0:T(4,128)S(1)} %get-tuple-element.64), channel_id=1, source_target_pairs={{4,0},{8,4},{12,8},{16,12},{20,16},{24,20},{28,24},{5,1},{9,5},{13... | collective-permute-start | bytes 18440 | tf_op jit(solution)/shard_map/ppermute | solution.py:21
  268.7 5.3 %collective-permute-start.37 = (f32[3,1,4,128]{3,2,1,0:T(4,128)S(1)}, f32[3,1,4,128]{3,2,1,0:T(4,128)S(1)}, u32[]{:S(2)}, u32[]{:S(2)}) collective-permute-start(f32[3,1,4,128]{3,2,1,0:T(4,128)S(1)} %get-tuple-element.63), channel_id=1, source_target_pairs={{0,4},{4,8},{8,12},{12,16},{16,20},{20,24},{24,28},{1,5},{5,9},{9,... | collective-permute-start | bytes 18440 | tf_op jit(solution)/shard_map/ppermute | solution.py:20
  274.0 5.0 %collective-permute-start.39 = (f32[3,4,1,128]{3,2,1,0:T(1,128)S(1)}, f32[3,4,1,128]{3,2,1,0:T(1,128)S(1)}, u32[]{:S(2)}, u32[]{:S(2)}) collective-permute-start(f32[3,4,1,128]{3,2,1,0:T(1,128)S(1)} %get-tuple-element.54), channel_id=1, source_target_pairs={{0,1},{1,2},{2,3},{4,5},{5,6},{6,7},{8,9},{9,10},{10,11},{12,13},{... | collective-permute-start | bytes 18440 | tf_op jit(solution)/shard_map/ppermute | solution.py:20
  277.1 4.9 %collective-permute-start.38 = (f32[3,4,1,128]{3,2,1,0:T(1,128)S(1)}, f32[3,4,1,128]{3,2,1,0:T(1,128)S(1)}, u32[]{:S(2)}, u32[]{:S(2)}) collective-permute-start(f32[3,4,1,128]{3,2,1,0:T(1,128)S(1)} %get-tuple-element.53), channel_id=1, source_target_pairs={{1,0},{2,1},{3,2},{5,4},{6,5},{7,6},{9,8},{10,9},{11,10},{13,12},{... | collective-permute-start | bytes 18440 | tf_op jit(solution)/shard_map/ppermute | solution.py:21
  291.8 5.3 %collective-permute-start.41 = (f32[3,2,8,256]{3,2,1,0:T(8,128)S(1)}, f32[3,2,8,256]{3,2,1,0:T(8,128)S(1)}, u32[]{:S(2)}, u32[]{:S(2)}) collective-permute-start(f32[3,2,8,256]{3,2,1,0:T(8,128)S(1)} %get-tuple-element.44), channel_id=1, source_target_pairs={{4,0},{8,4},{12,8},{16,12},{20,16},{24,20},{28,24},{5,1},{9,5},{13... | collective-permute-start | bytes 147464 | tf_op jit(solution)/shard_map/ppermute | solution.py:21
  293.7 5.7 %collective-permute-start.40 = (f32[3,2,8,256]{3,2,1,0:T(8,128)S(1)}, f32[3,2,8,256]{3,2,1,0:T(8,128)S(1)}, u32[]{:S(2)}, u32[]{:S(2)}) collective-permute-start(f32[3,2,8,256]{3,2,1,0:T(8,128)S(1)} %get-tuple-element.43), channel_id=1, source_target_pairs={{0,4},{4,8},{8,12},{12,16},{16,20},{20,24},{24,28},{1,5},{5,9},{9,... | collective-permute-start | bytes 147464 | tf_op jit(solution)/shard_map/ppermute | solution.py:20
  299.5 5.8 %collective-permute-start.43 = (f32[3,8,2,256]{3,1,2,0:T(8,128)S(1)}, f32[3,8,2,256]{3,1,2,0:T(8,128)S(1)}, u32[]{:S(2)}, u32[]{:S(2)}) collective-permute-start(f32[3,8,2,256]{3,1,2,0:T(8,128)S(1)} %copy.208), channel_id=1, source_target_pairs={{1,0},{2,1},{3,2},{5,4},{6,5},{7,6},{9,8},{10,9},{11,10},{13,12},{... | collective-permute-start | bytes 147464 | tf_op jit(solution)/shard_map/ppermute | solution.py:21
  301.5 4.8 %collective-permute-start.42 = (f32[3,8,2,256]{3,1,2,0:T(8,128)S(1)}, f32[3,8,2,256]{3,1,2,0:T(8,128)S(1)}, u32[]{:S(2)}, u32[]{:S(2)}) collective-permute-start(f32[3,8,2,256]{3,1,2,0:T(8,128)S(1)} %copy.207), channel_id=1, source_target_pairs={{0,1},{1,2},{2,3},{4,5},{5,6},{6,7},{8,9},{9,10},{10,11},{12,13},{... | collective-permute-start | bytes 147464 | tf_op jit(solution)/shard_map/ppermute | solution.py:20
  319.5 11.7 %collective-permute-start.45 = (f32[3,2,16,512]{3,2,1,0:T(8,128)S(1)}, f32[3,2,16,512]{3,2,1,0:T(8,128)S(1)}, u32[]{:S(2)}, u32[]{:S(2)}) collective-permute-start(f32[3,2,16,512]{3,2,1,0:T(8,128)S(1)} %get-tuple-element.26), channel_id=1, source_target_pairs={{4,0},{8,4},{12,8},{16,12},{20,16},{24,20},{28,24},{5,1},{9,5},{13... | collective-permute-start | bytes 589832 | tf_op jit(solution)/shard_map/ppermute | solution.py:21
  321.5 9.7 %collective-permute-start.44 = (f32[3,2,16,512]{3,2,1,0:T(8,128)S(1)}, f32[3,2,16,512]{3,2,1,0:T(8,128)S(1)}, u32[]{:S(2)}, u32[]{:S(2)}) collective-permute-start(f32[3,2,16,512]{3,2,1,0:T(8,128)S(1)} %get-tuple-element.25), channel_id=1, source_target_pairs={{0,4},{4,8},{8,12},{12,16},{16,20},{20,24},{24,28},{1,5},{5,9},{9,... | collective-permute-start | bytes 589832 | tf_op jit(solution)/shard_map/ppermute | solution.py:20
  331.3 6.8 %collective-permute-start.47 = (f32[3,12,2,512]{3,2,1,0:T(2,128)S(1)}, f32[3,12,2,512]{3,2,1,0:T(2,128)S(1)}, u32[]{:S(2)}, u32[]{:S(2)}) collective-permute-start(f32[3,12,2,512]{3,2,1,0:T(2,128)S(1)} %get-tuple-element.24), channel_id=1, source_target_pairs={{1,0},{2,1},{3,2},{5,4},{6,5},{7,6},{9,8},{10,9},{11,10},{13,12},{... | collective-permute-start | bytes 442376 | tf_op jit(solution)/shard_map/ppermute | solution.py:21
  333.4 5.9 %collective-permute-start.46 = (f32[3,12,2,512]{3,2,1,0:T(2,128)S(1)}, f32[3,12,2,512]{3,2,1,0:T(2,128)S(1)}, u32[]{:S(2)}, u32[]{:S(2)}) collective-permute-start(f32[3,12,2,512]{3,2,1,0:T(2,128)S(1)} %get-tuple-element.23), channel_id=1, source_target_pairs={{0,1},{1,2},{2,3},{4,5},{5,6},{6,7},{8,9},{9,10},{10,11},{12,13},{... | collective-permute-start | bytes 442376 | tf_op jit(solution)/shard_map/ppermute | solution.py:20
  (63 other events, 924.3 us)
where the time goes:
time: 353 us; the launch traced here: 349 us
  starting transfers between devices  137 us (39%)
  local copies, waits for them, and re-layouts  106 us (30%)
  other arithmetic  54.4 us (15%)
  waiting for transfers between devices  49.6 us (14%)
    ppermute x24, starting transfers between devices, extended(): before = lax.ppermute(last, axis, up)  80.5 us
    reshape x3, local copies, waits for them, and re-layouts, restrict(): values.reshape(leading + (extent[-3] // 2, 2, extent[-2] // 2, 2, extent[...  78.1 us
    ppermute x24, starting transfers between devices, extended(): after = lax.ppermute(initial, axis, down)  56.2 us
    reduce_sum x4, other arithmetic, restrict(): return jnp.mean(blocks, axis=(-5, -3, -1))  28.3 us
    ppermute x24, waiting for transfers between devices, extended(): before = lax.ppermute(last, axis, up)  27.7 us
    ppermute x24, waiting for transfers between devices, extended(): after = lax.ppermute(initial, axis, down)  21.9 us
    broadcast_in_dim x2, local copies, waits for them, and re-layouts, prolong(): jnp.repeat(jnp.repeat(jnp.repeat(values, 2, axis=-3), 2, axis=-2), 2, axi...  7.69 us
  transfers between devices with their start and end apart: 48, of which 21 were waited for; matrix products, arithmetic and copies ran while one was open for 31% of the time, Pallas kernels for 0%

commit v1 on v0

v1 whole, which is shorter than its diff:
```python
import functools

import jax
import jax.numpy as jnp
from jax import lax
from jax.experimental import pallas as pl
from jax.experimental.pallas import tpu as pltpu
from jax.sharding import PartitionSpec as P

COARSE_SWEEPS = 6
VISCOSITIES = (0.2, 0.6, 1.5, 4.0)
WEIGHT = 2.0 / 3.0
MESH = pl.DeviceIdType.MESH
WINDOW = [(dx, dy) for dx in range(-2, 3) for dy in range(-1, 2) if (dx, dy) != (0, 0)]
TOP = 8


def up8(n):
    return -(-n // 8) * 8


def side_slices(step, first, length, lo, hi):
    if step > 0:
        return (first + length - hi, first - hi)
    return (first + lo - 1, first + length + lo - 1)


class Kernel:
    def __init__(self, sizes, comps, grid):
        self.X, self.Y, self.Z = sizes
        self.C = comps
        self.grid = grid
        self.scratch = {}
        self.n_sems = 0
        self.plan()

    def buf(self, name, shape, dtype=jnp.float32):
        self.scratch[name] = pltpu.VMEM(tuple(shape), dtype)

    def halo(self, name, target, comps, px, X, Y, Z, lo, hi, diag):
        w = hi - lo + 1
        msgs = []
        for dx in (1, -1):
            s, d = side_slices(dx, px, X, lo, hi)
            msgs.append(("x", dx, 0, s, d, self.n_sems))
            self.n_sems += 1
        n = comps * X * w
        self.buf(name + "_sy", (2, up8(n), Z))
        self.buf(name + "_ry", (2, up8(n), Z))
        for k, dy in enumerate((1, -1)):
            s, d = side_slices(dy, TOP, Y, lo, hi)
            msgs.append(("y", k, dy, s, d, self.n_sems))
            self.n_sems += 1
        if diag:
            n = comps * diag * diag
            self.buf(name + "_sd", (4, up8(n), Z))
            self.buf(name + "_rd", (4, up8(n), Z))
            for k, (dx, dy) in enumerate([(1, 1), (1, -1), (-1, 1), (-1, -1)]):
                msgs.append(("d", k, (dx, dy), side_slices(dx, px, X, 1, diag),
                             side_slices(dy, TOP, Y, 1, diag), self.n_sems))
                self.n_sems += 1
        return dict(name=name, target=target, comps=comps, px=px, X=X, Y=Y, w=w, diag=diag, msgs=msgs)

    def plan(self):
        X, Y, Z, C = self.X, self.Y, self.Z, self.C
        self.P0, self.R0 = X + 4, Y + 16
        self.X1, self.Y1, self.Z1 = X // 2, Y // 2, Z // 2
        self.P1, self.R1 = self.X1 + 6, self.Y1 + 16
        self.X2, self.Y2, self.Z2 = X // 4, Y // 4, Z // 4
        self.P2, self.R2 = self.X2 + 8, up8(self.Y2 * 3)
        b = self.buf
        b("ph", (X, Y, Z), jnp.int32)
        b("E0", (1, self.P0, self.R0, Z))
        b("C0", (8, self.P0, self.R0, Z))
        for n in ("F0", "A0", "V0", "B0"):
            b(n, (C, self.P0, self.R0, Z))
        b("O0", (C, X, Y, Z))
        b("T0", (C * self.X1 * Y, Z))
        b("E1", (1, self.P1, self.R1, self.Z1))
        b("C1", (8, self.P1, self.R1, self.Z1))
        for n in ("F1", "A1", "V1", "B1"):
            b(n, (C, self.P1, self.R1, self.Z1))
        b("T1", (C * self.X2 * self.Y1, self.Z1))
        b("E2", (1, self.P2, self.R2, self.Z2))
        b("C2", (8, self.P2, self.R2, self.Z2))
        for n in ("F2", "A2", "B2"):
            b(n, (C, self.P2, self.R2, self.Z2))
        blk = self.X2 * self.Y2
        for n, c in (("e2", 1), ("f2", C), ("v2", C)):
            b("S" + n, (c * blk, self.Z2))
            b("R" + n, (len(WINDOW), c * blk, self.Z2))
        b("UZ1", (self.R2 * C * (self.X2 + 4), self.Z1))
        b("UZ0", (self.R1 * C * (self.X1 + 2), self.Z))
        self.hE0 = self.halo("hE0", "E0", 1, 2, X, Y, Z, 1, 2, 1)
        self.hF0 = self.halo("hF0", "F0", C, 2, X, Y, Z, 1, 1, 0)
        self.hV0 = self.halo("hV0", "V0", C, 2, X, Y, Z, 1, 1, 0)
        self.hW0 = self.halo("hW0", "V0", C, 2, X, Y, Z, 2, 2, 1)
        self.hE1 = self.halo("hE1", "E1", 1, 3, self.X1, self.Y1, self.Z1, 1, 3, 3)
        self.hF1 = self.halo("hF1", "F1", C, 3, self.X1, self.Y1, self.Z1, 1, 2, 2)
        self.hV1 = self.halo("hV1", "V1", C, 3, self.X1, self.Y1, self.Z1, 1, 3, 3)
        self.win = {}
        for n in ("e2", "f2", "v2"):
            self.win[n] = self.n_sems
            self.n_sems += len(WINDOW)

    def exists(self, dx, dy):
        ok = None
        for step, me, size in ((dx, self.gx, self.grid[0]), (dy, self.gy, self.grid[1])):
            if step:
                t = (me + step >= 0) & (me + step < size)
                ok = t if ok is None else ok & t
        return ok

    def copy(self, src, dst, sem, dx, dy):
        return pltpu.make_async_remote_copy(
            src_ref=src, dst_ref=dst, send_sem=self.ssem.at[sem], recv_sem=self.rsem.at[sem],
            device_id=(self.gx + dx, self.gy + dy), device_id_type=MESH)

    def halo_copies(self, h):
        r = self.r
        ref = r[h["target"]]
        rows = pl.ds(TOP, h["Y"])
        out = []
        for m in h["msgs"]:
            if m[0] == "x":
                _, dx, dy, s, d, sem = m
                c = self.copy(ref.at[:, pl.ds(s, h["w"]), rows, :], ref.at[:, pl.ds(d, h["w"]), rows, :], sem, dx, 0)
                out.append((c, dx, 0))
            elif m[0] == "y":
                _, k, dy, s, d, sem = m
                out.append((self.copy(r[h["name"] + "_sy"].at[k], r[h["name"] + "_ry"].at[k], sem, 0, dy), 0, dy))
            else:
                _, k, (dx, dy), _, _, sem = m
                out.append((self.copy(r[h["name"] + "_sd"].at[k], r[h["name"] + "_rd"].at[k], sem, dx, dy), dx, dy))
        return out

    def rows_of(self, h, m, which):
        if m[0] == "y":
            start = m[3 + which]
            return m[1], "y", [(c, h["px"] + p, start + q) for c in range(h["comps"])
                               for p in range(h["X"]) for q in range(h["w"])]
        g = h["diag"]
        return m[1], "d", [(c, m[3][which] + p, m[4][which] + q) for c in range(h["comps"])
                           for p in range(g) for q in range(g)]

    def halo_start(self, h):
        ref = self.r[h["target"]]
        for m in h["msgs"]:
            if m[0] == "x":
                continue
            k, kind, rows = self.rows_of(h, m, 0)
            stage = self.r[h["name"] + "_s" + kind]
            for i, (c, p, q) in enumerate(rows):
                stage[k, i:i + 1, :] = ref[c, p, q:q + 1, :]
        for c, dx, dy in self.halo_copies(h):
            pl.when(self.exists(dx, dy))(c.start)

    def halo_wait(self, h):
        ref = self.r[h["target"]]
        copies = self.halo_copies(h)
        for c, dx, dy in copies:
            pl.when(self.exists(-dx, -dy))(c.wait_recv)
        for m in h["msgs"]:
            if m[0] == "x":
                continue
            k, kind, rows = self.rows_of(h, m, 1)
            stage = self.r[h["name"] + "_r" + kind]
            for i, (c, p, q) in enumerate(rows):
                ref[c, p, q:q + 1, :] = stage[k, i:i + 1, :]

    def halo_sent(self, h):
        for c, dx, dy in self.halo_copies(h):
            pl.when(self.exists(dx, dy))(c.wait_send)

    def win_copies(self, n):
        src, dst = self.r["S" + n], self.r["R" + n]
        return [(self.copy(src, dst.at[k], self.win[n] + k, dx, dy), dx, dy) for k, (dx, dy) in enumerate(WINDOW)]

    def win_start(self, n):
        for c, dx, dy in self.win_copies(n):
            pl.when(self.exists(dx, dy))(c.start)

    def win_wait(self, n, target):
        copies = self.win_copies(n)
        for c, dx, dy in copies:
            pl.when(self.exists(-dx, -dy))(c.wait_recv)
        ref = self.r[target]
        X2, Y2 = self.X2, self.Y2
        for k, (dx, dy) in enumerate(WINDOW + [(0, 0)]):
            for c in range(ref.shape[0]):
                for p in range(X2):
                    i = (c * X2 + p) * Y2
                    if (dx, dy) == (0, 0):
                        v = self.r["S" + n][i:i + Y2, :]
                    else:
                        v = self.r["R" + n][k, i:i + Y2, :]
                    ref[c, 4 + p - dx * X2, Y2 * (1 - dy):Y2 * (2 - dy), :] = v

    def win_sent(self, n):
        for c, dx, dy in self.win_copies(n):
            pl.when(self.exists(dx, dy))(c.wait_send)

    def coefs(self, E, K, a, b, scale):
        E, K = self.r[E], self.r[K]
        Z = E.shape[-1]
        shape = E.shape[-2:]
        R = shape[0]
        s = 1.0 / scale

        @pl.loop(a, b)
        def _(i):
            z = lax.broadcasted_iota(jnp.int32, shape, 1)
            e = E[0, i]

            def face(o):
                t = e + o
                return jnp.where(jnp.minimum(e, o) > 0.0, t * (0.5 * s), t * s)

            zp = jnp.where(z == Z - 1, 0.0, pltpu.roll(e, Z - 1, 1))
            zm = jnp.where(z == 0, 0.0, pltpu.roll(e, 1, 1))
            others = (E[0, i + 1], E[0, i - 1], pltpu.roll(e, R - 1, 0), pltpu.roll(e, 1, 0), zp, zm)
            diag = None
            for k, o in enumerate(others):
                c = face(o)
                diag = c if diag is None else diag + c
                if k == 4:
                    c = jnp.where(z == Z - 1, 0.0, c)
                if k == 5:
                    c = jnp.where(z == 0, 0.0, c)
                K[k, i] = c
            inside = e > 0.0
            K[6, i] = jnp.where(inside, WEIGHT / jnp.where(inside, diag, 1.0), 0.0)
            K[7, i] = diag

    def stencil(self, V, K, G, i, c, rows):
        R, Z = V.shape[-2:]
        n = rows.stop - rows.start
        v = V[c, i, rows, :]
        if n == R:
            yp, ym = pltpu.roll(v, R - 1, 0), pltpu.roll(v, 1, 0)
        else:
            yp, ym = V[c, i, rows.start + 1:rows.stop + 1, :], V[c, i, rows.start - 1:rows.stop - 1, :]
        acc = G[c, i, rows, :]
        parts = (V[c, i + 1, rows, :], V[c, i - 1, rows, :], yp, ym, pltpu.roll(v, Z - 1, 1), pltpu.roll(v, 1, 1))
        for k, o in enumerate(parts):
            acc = acc + K[k, i, rows, :] * o
        return v, acc

    def first(self, K, G, O, a, b):
        K, G, O = (self.r[n] for n in (K, G, O))

        @pl.loop(a, b)
        def _(i):
            w = K[6, i]
            for c in range(self.C):
                O[c, i] = w * G[c, i]

    def sweep(self, V, K, G, O, a, b, rows=None, shift=0):
        V, K, G, O = (self.r[n] for n in (V, K, G, O))
        rows = rows or slice(0, V.shape[-2])
        out_rows = rows if shift == 0 else slice(0, rows.stop - rows.start)

        @pl.loop(a, b)
        def _(i):
            for c in range(self.C):
                v, acc = self.stencil(V, K, G, i, c, rows)
                O[c, i - shift, out_rows, :] = (1.0 - WEIGHT) * v + K[6, i, rows, :] * acc

    def residual(self, V, K, G, T, px, Xc, Y):
        V, K, G, T = (self.r[n] for n in (V, K, G, T))
        rows = slice(TOP, TOP + Y)

        @pl.loop(0, Xc)
        def _(j):
            for c in range(self.C):
                total = None
                for q in range(2):
                    i = px + 2 * j + q
                    v, acc = self.stencil(V, K, G, i, c, rows)
                    d = acc - K[7, i, rows, :] * v
                    total = d if total is None else total + d
                T[pl.ds(pl.multiple_of((c * Xc + j) * Y, 8), Y), :] = 0.5 * total

    def dot(self, a, b):
        return lax.dot_general(a, b, (((1,), (0,)), ((), ())), precision=lax.Precision.HIGHEST,
                               preferred_element_type=jnp.float32)

    def pairs(self, n, m, value, fine_dim):
        r = lax.broadcasted_iota(jnp.int32, (n, m), 0)
        c = lax.broadcasted_iota(jnp.int32, (n, m), 1)
        hit = (r >> 1) == c if fine_dim == 0 else (c >> 1) == r
        return jnp.where(hit, value, 0.0).astype(jnp.float32)

    def squeeze(self, t):
        rows, Z = t.shape
        half = self.dot(t, self.pairs(Z, Z // 2, 0.5, 0))
        return self.dot(self.pairs(rows // 2, rows, 0.5, 1), half)

    def prolong(self, W, a, count, U, V, planes, coarse_of, offset):
        W, U, V = (self.r[n] for n in (W, U, V))
        C, _, Rc, Zc = W.shape
        Rf, Zf = V.shape[-2:]
        src = W[:, a:a + count].reshape(C * count * Rc, Zc)
        U[...] = self.dot(src, self.pairs(Zf, Zc, 1.0, 0).T if False else self.pairs(Zc, Zf, 1.0, 1))
        r = lax.broadcasted_iota(jnp.int32, (Rf, Rc), 0)
        c = lax.broadcasted_iota(jnp.int32, (Rf, Rc), 1)
        lift = jnp.where(((r + 2 * offset - TOP) >> 1) == c, 1.0, 0.0).astype(jnp.float32)
        for comp in range(C):
            for k in range(count):
                start = (comp * count + k) * Rc
                block = self.dot(lift, U[start:start + Rc, :])
                for p in planes:
                    if coarse_of(p) == a + k:
                        V[comp, p] = V[comp, p] + block

    def body(self, forcing, phase, out, *scratch):
        names = list(self.scratch)
        self.r = r = dict(zip(names, scratch))
        self.ssem, self.rsem, lsem = scratch[len(names):]
        self.gx, self.gy = lax.axis_index("gx"), lax.axis_index("gy")
        X, Y, Z, C = self.X, self.Y, self.Z, self.C
        X1, Y1 = self.X1, self.Y1
        block = (pl.ds(2, X), pl.ds(TOP, Y))
        load_p = pltpu.make_async_copy(phase, r["ph"], lsem.at[0])
        load_p.start()
        for n in ("E0", "F0", "V0", "E1", "F1", "V1", "E2", "F2", "A2"):
            ref = r[n]
            for c in range(ref.shape[0]):
                @pl.loop(0, ref.shape[1])
                def _(i):
                    ref[c, i] = jnp.zeros(ref.shape[2:], jnp.float32)
        for n in list(r):
            if n.startswith("h") and n[-3:] in ("_ry", "_rd") or n in ("Re2", "Rf2", "Rv2"):
                ref = r[n]
                for k in range(ref.shape[0]):
                    ref[k] = jnp.zeros(ref.shape[1:], jnp.float32)
        load_f = pltpu.make_async_copy(forcing, r["F0"].at[:, block[0], block[1], :], lsem.at[1])
        load_f.start()

        barrier = pltpu.get_barrier_semaphore()
        count = jnp.int32(0)
        for dx, dy in WINDOW:
            ok = self.exists(dx, dy)
            count = count + ok.astype(jnp.int32)

            @pl.when(ok)
            def _():
                pl.semaphore_signal(barrier, inc=1, device_id=(self.gx + dx, self.gy + dy), device_id_type=MESH)
        load_p.wait()

        @pl.loop(0, X)
        def _(i):
            ph = r["ph"][i]
            e = jnp.zeros(ph.shape, jnp.float32)
            for k, value in enumerate(VISCOSITIES):
                e = jnp.where(ph == k, jnp.float32(value), e)
            r["E0"][0, i + 2, TOP:TOP + Y, :] = e
        pl.semaphore_wait(barrier, count)
        self.halo_start(self.hE0)
        load_f.wait()
        self.halo_start(self.hF0)

        for j in range(X1):
            r["T0"][j * Y:(j + 1) * Y, :] = 0.5 * (
                r["E0"][0, 2 + 2 * j, TOP:TOP + Y, :] + r["E0"][0, 3 + 2 * j, TOP:TOP + Y, :])
        e1 = self.squeeze(r["T0"][0:X1 * Y, :])
        for j in range(X1):
            r["E1"][0, 3 + j, TOP:TOP + Y1, :] = e1[j * Y1:(j + 1) * Y1]
        self.halo_start(self.hE1)
        for j in range(self.X2):
            r["T1"][j * Y1:(j + 1) * Y1, :] = 0.5 * (
                e1[2 * j * Y1:(2 * j + 1) * Y1] + e1[(2 * j + 1) * Y1:(2 * j + 2) * Y1])
        r["Se2"][...] = self.squeeze(r["T1"][0:self.X2 * Y1, :])
        self.win_start("e2")

        self.halo_wait(self.hE0)
        self.coefs("E0", "C0", 1, X + 3, 1.0)
        self.halo_wait(self.hF0)
        self.first("C0", "F0", "A0", 1, X + 3)
        rows0 = slice(TOP, TOP + Y)
        self.sweep("A0", "C0", "F0", "V0", 2, X + 2, rows0)
        self.halo_start(self.hV0)
        self.halo_wait(self.hE1)
        self.coefs("E1", "C1", 1, X1 + 5, 4.0)
        self.win_wait("e2", "E2")
        self.coefs("E2", "C2", 1, self.X2 + 7, 16.0)
        self.halo_wait(self.hV0)
        self.residual("V0", "C0", "F0", "T0", 2, X1, Y)
        f1 = self.squeeze(r["T0"][...])
        for c in range(C):
            for j in range(X1):
                s = (c * X1 + j) * Y1
                r["F1"][c, 3 + j, TOP:TOP + Y1, :] = f1[s:s + Y1]

        self.halo_start(self.hF1)
        self.halo_wait(self.hF1)
        self.halo_start(self.hW0)
        self.first("C1", "F1", "A1", 1, X1 + 5)
        self.sweep("A1", "C1", "F1", "B1", 2, X1 + 4)
        self.residual("B1", "C1", "F1", "T1", 3, self.X2, Y1)
        r["Sf2"][...] = self.squeeze(r["T1"][...])
        self.win_start("f2")
        for c in range(C):
            for j in range(X1):
                r["V1"][c, 3 + j, TOP:TOP + Y1, :] = r["B1"][c, 3 + j, TOP:TOP + Y1, :]
        self.halo_start(self.hV1)

        self.win_wait("f2", "F2")
        p2 = self.P2
        self.first("C2", "F2", "A2", 1, p2 - 1)
        self.sweep("A2", "C2", "F2", "B2", 2, p2 - 2)
        self.sweep("B2", "C2", "F2", "A2", 3, p2 - 3)
        self.sweep("A2", "C2", "F2", "B2", 4, p2 - 4)
        for c in range(C):
            for p in range(self.X2):
                i = (c * self.X2 + p) * self.Y2
                r["Sv2"][i:i + self.Y2, :] = r["B2"][c, 4 + p, self.Y2:2 * self.Y2, :]
        self.win_start("v2")
        self.win_wait("v2", "A2")
        self.sweep("A2", "C2", "F2", "B2", 1, p2 - 1)
        self.sweep("B2", "C2", "F2", "A2", 2, p2 - 2)

        self.halo_wait(self.hV1)
        self.halo_sent(self.hV1)
        self.prolong("A2", 2, self.X2 + 4, "UZ1", "V1", range(self.P1),
                     lambda p: 4 + (p - 3) // 2, self.Y2)
        self.sweep("V1", "C1", "F1", "A1", 1, X1 + 5)
        self.sweep("A1", "C1", "F1", "B1", 2, X1 + 4)

        self.halo_wait(self.hW0)
        self.halo_sent(self.hV0)
        self.halo_sent(self.hW0)
        self.prolong("B1", 2, X1 + 2, "UZ0", "V0", range(self.P0),
                     lambda p: 3 + (p - 2) // 2, TOP)
        self.sweep("V0", "C0", "F0", "B0", 1, X + 3)
        self.sweep("B0", "C0", "F0", "O0", 2, X + 2, rows0, shift=2)
        store = pltpu.make_async_copy(r["O0"], out, lsem.at[0])
        store.start()
        for h in (self.hE0, self.hF0, self.hE1, self.hF1):
            self.halo_sent(h)
        for n in ("e2", "f2", "v2"):
            self.win_sent(n)
        store.wait()

    def __call__(self, forcing, phase):
        any_space = pl.BlockSpec(memory_space=pl.ANY)
        sems = [pltpu.SemaphoreType.DMA((self.n_sems,)), pltpu.SemaphoreType.DMA((self.n_sems,)),
                pltpu.SemaphoreType.DMA((2,))]
        return pl.pallas_call(
            self.body,
            out_shape=jax.ShapeDtypeStruct(forcing.shape, jnp.float32),
            in_specs=[any_space, any_space],
            out_specs=any_space,
            scratch_shapes=list(self.scratch.values()) + sems,
            compiler_params=pltpu.CompilerParams(
                collective_id=0, has_side_effects=True, vmem_limit_bytes=60 * 1024 * 1024),
            name="vcycle",
        )(forcing, phase)


def solution(mesh):
    grid = (mesh.shape["gx"], mesh.shape["gy"])

    def per_device(forcing, phase_ids):
        return Kernel(phase_ids.shape, forcing.shape[0], grid)(forcing, phase_ids)

    return jax.shard_map(
        per_device,
        mesh=mesh,
        in_specs=(P(None, "gx", "gy", None), P("gx", "gy", None)),
        out_specs=P(None, "gx", "gy", None),
        check_vma=False,
    )
```

time: 353 us -> 60.3 us (0.17)
  the two profiles are of different devices: /device:TPU:17 before, /device:TPU:1 now
where the time goes in v1:
time: 60.3 us; the launch traced here: 60.2 us
  Pallas kernels  58.1 us (96%)
  local copies, waits for them, and re-layouts  2.09 us (3%)
    pallas_call x1, Pallas kernels, __call__(): pl.pallas_call(self.body, out_shape=jax.ShapeDtypeStruct(forcing.shape, j...  58.1 us
    unnamed x1, local copies, waits for them, and re-layouts  2.09 us

profile of v1, /device:TPU:1, one launch (start us, length us, event | category | flops | bytes accessed | tf_op | source)
XLA Modules:
  0.0 60.2 jit_solution(15418303589307967000)
XLA Ops:
  0.0 58.1 %vcycle.1 = f32[3,8,16,512]{3,2,1,0:T(8,128)} custom-call(f32[3,8,16,512]{3,2,1,0:T(8,128)} %forcing.1, s32[8,16,512]{2,1,0:T(8,128)} %phase.1), custom_call_target="tpu_custom_call" | custom-call | tf_op jit(solution)/shard_map/vcycle/pallas_call | solution.py:449
  58.1 2.1 %copy.4 = f32[3,8,16,512]{3,2,1,0:T(8,128)} copy(f32[3,8,16,512]{3,2,1,0:T(8,128)} %vcycle.1) | data formatting | bytes 1572864

commit v2 on v1

--- a/solution.py
+++ b/solution.py
@@ -37,7 +37,7 @@
     def buf(self, name, shape, dtype=jnp.float32):
         self.scratch[name] = pltpu.VMEM(tuple(shape), dtype)
 
-    def halo(self, name, target, comps, px, X, Y, Z, lo, hi, diag):
+    def halo(self, name, target, comps, px, X, Y, Z, lo, hi, diag, base=0):
         w = hi - lo + 1
         msgs = []
         for dx in (1, -1):
@@ -52,14 +52,19 @@
             msgs.append(("y", k, dy, s, d, self.n_sems))
             self.n_sems += 1
         if diag:
-            n = comps * diag * diag
+            n = comps * len(diag)
             self.buf(name + "_sd", (4, up8(n), Z))
             self.buf(name + "_rd", (4, up8(n), Z))
             for k, (dx, dy) in enumerate([(1, 1), (1, -1), (-1, 1), (-1, -1)]):
-                msgs.append(("d", k, (dx, dy), side_slices(dx, px, X, 1, diag),
-                             side_slices(dy, TOP, Y, 1, diag), self.n_sems))
+                cells = [[], []]
+                for a, b in diag:
+                    sx, tx = side_slices(dx, px, X, a, a)
+                    sy, ty = side_slices(dy, TOP, Y, b, b)
+                    cells[0].append((sx, sy))
+                    cells[1].append((tx, ty))
+                msgs.append(("d", k, (dx, dy), cells[0], cells[1], self.n_sems))
                 self.n_sems += 1
-        return dict(name=name, target=target, comps=comps, px=px, X=X, Y=Y, w=w, diag=diag, msgs=msgs)
+        return dict(name=name, base=base, target=target, comps=comps, px=px, X=X, Y=Y, w=w, diag=diag, msgs=msgs)
 
     def plan(self):
         X, Y, Z, C = self.X, self.Y, self.Z, self.C
@@ -91,13 +96,14 @@
             b("R" + n, (len(WINDOW), c * blk, self.Z2))
         b("UZ1", (self.R2 * C * (self.X2 + 4), self.Z1))
         b("UZ0", (self.R1 * C * (self.X1 + 2), self.Z))
-        self.hE0 = self.halo("hE0", "E0", 1, 2, X, Y, Z, 1, 2, 1)
-        self.hF0 = self.halo("hF0", "F0", C, 2, X, Y, Z, 1, 1, 0)
-        self.hV0 = self.halo("hV0", "V0", C, 2, X, Y, Z, 1, 1, 0)
-        self.hW0 = self.halo("hW0", "V0", C, 2, X, Y, Z, 2, 2, 1)
-        self.hE1 = self.halo("hE1", "E1", 1, 3, self.X1, self.Y1, self.Z1, 1, 3, 3)
-        self.hF1 = self.halo("hF1", "F1", C, 3, self.X1, self.Y1, self.Z1, 1, 2, 2)
-        self.hV1 = self.halo("hV1", "V1", C, 3, self.X1, self.Y1, self.Z1, 1, 3, 3)
+        reach = [(1, 1), (1, 2), (2, 1), (1, 3), (2, 2), (3, 1)]
+        self.hE0 = self.halo("hE0", "E0", 1, 2, X, Y, Z, 1, 2, [(1, 1)])
+        self.hF0 = self.halo("hF0", "F0", C, 2, X, Y, Z, 1, 1, [])
+        self.hV0 = self.halo("hV0", "V0", C, 2, X, Y, Z, 1, 1, [])
+        self.hW0 = [self.halo("hW%d" % c, "V0", 1, 2, X, Y, Z, 2, 2, [(1, 1)], c) for c in range(C)]
+        self.hE1 = self.halo("hE1", "E1", 1, 3, self.X1, self.Y1, self.Z1, 1, 3, reach)
+        self.hF1 = self.halo("hF1", "F1", C, 3, self.X1, self.Y1, self.Z1, 1, 2, reach[:3])
+        self.hV1 = self.halo("hV1", "V1", C, 3, self.X1, self.Y1, self.Z1, 2, 3, reach[1:])
         self.win = {}
         for n in ("e2", "f2", "v2"):
             self.win[n] = self.n_sems
@@ -116,15 +122,19 @@
             src_ref=src, dst_ref=dst, send_sem=self.ssem.at[sem], recv_sem=self.rsem.at[sem],
             device_id=(self.gx + dx, self.gy + dy), device_id_type=MESH)
 
-    def halo_copies(self, h):
+    def halo_copies(self, h, kinds="xyd"):
         r = self.r
         ref = r[h["target"]]
         rows = pl.ds(TOP, h["Y"])
         out = []
         for m in h["msgs"]:
+            if m[0] not in kinds:
+                continue
             if m[0] == "x":
                 _, dx, dy, s, d, sem = m
-                c = self.copy(ref.at[:, pl.ds(s, h["w"]), rows, :], ref.at[:, pl.ds(d, h["w"]), rows, :], sem, dx, 0)
+                comps = pl.ds(h["base"], h["comps"])
+                c = self.copy(ref.at[comps, pl.ds(s, h["w"]), rows, :], ref.at[comps, pl.ds(d, h["w"]), rows, :],
+                              sem, dx, 0)
                 out.append((c, dx, 0))
             elif m[0] == "y":
                 _, k, dy, s, d, sem = m
@@ -137,31 +147,28 @@
     def rows_of(self, h, m, which):
         if m[0] == "y":
             start = m[3 + which]
-            return m[1], "y", [(c, h["px"] + p, start + q) for c in range(h["comps"])
+            return m[1], "y", [(c + h["base"], h["px"] + p, start + q) for c in range(h["comps"])
                                for p in range(h["X"]) for q in range(h["w"])]
-        g = h["diag"]
-        return m[1], "d", [(c, m[3][which] + p, m[4][which] + q) for c in range(h["comps"])
-                           for p in range(g) for q in range(g)]
-
-    def halo_start(self, h):
+        return m[1], "d", [(c + h["base"], p, q) for c in range(h["comps"]) for p, q in m[3 + which]]
+
+    def halo_start(self, h, kinds="xyd"):
         ref = self.r[h["target"]]
         for m in h["msgs"]:
-            if m[0] == "x":
+            if m[0] == "x" or m[0] not in kinds:
                 continue
             k, kind, rows = self.rows_of(h, m, 0)
             stage = self.r[h["name"] + "_s" + kind]
             for i, (c, p, q) in enumerate(rows):
                 stage[k, i:i + 1, :] = ref[c, p, q:q + 1, :]
-        for c, dx, dy in self.halo_copies(h):
+        for c, dx, dy in self.halo_copies(h, kinds):
             pl.when(self.exists(dx, dy))(c.start)
 
-    def halo_wait(self, h):
+    def halo_wait(self, h, kinds="xyd"):
         ref = self.r[h["target"]]
-        copies = self.halo_copies(h)
-        for c, dx, dy in copies:
+        for c, dx, dy in self.halo_copies(h, kinds):
             pl.when(self.exists(-dx, -dy))(c.wait_recv)
         for m in h["msgs"]:
-            if m[0] == "x":
+            if m[0] == "x" or m[0] not in kinds:
                 continue
             k, kind, rows = self.rows_of(h, m, 1)
             stage = self.r[h["name"] + "_r" + kind]
@@ -266,11 +273,11 @@
                 v, acc = self.stencil(V, K, G, i, c, rows)
                 O[c, i - shift, out_rows, :] = (1.0 - WEIGHT) * v + K[6, i, rows, :] * acc
 
-    def residual(self, V, K, G, T, px, Xc, Y):
+    def residual(self, V, K, G, T, px, Xc, Y, a=0, b=None):
         V, K, G, T = (self.r[n] for n in (V, K, G, T))
         rows = slice(TOP, TOP + Y)
 
-        @pl.loop(0, Xc)
+        @pl.loop(a, Xc if b is None else b)
         def _(j):
             for c in range(self.C):
                 total = None
@@ -373,19 +380,28 @@
         r["Se2"][...] = self.squeeze(r["T1"][0:self.X2 * Y1, :])
         self.win_start("e2")
 
-        self.halo_wait(self.hE0)
-        self.coefs("E0", "C0", 1, X + 3, 1.0)
+        self.halo_wait(self.hE0, "y")
+        self.coefs("E0", "C0", 3, X + 1, 1.0)
+        self.halo_wait(self.hE0, "xd")
+        self.coefs("E0", "C0", 1, 3, 1.0)
+        self.coefs("E0", "C0", X + 1, X + 3, 1.0)
         self.halo_wait(self.hF0)
         self.first("C0", "F0", "A0", 1, X + 3)
         rows0 = slice(TOP, TOP + Y)
-        self.sweep("A0", "C0", "F0", "V0", 2, X + 2, rows0)
-        self.halo_start(self.hV0)
+        self.sweep("A0", "C0", "F0", "V0", 2, 3, rows0)
+        self.sweep("A0", "C0", "F0", "V0", X + 1, X + 2, rows0)
+        self.halo_start(self.hV0, "x")
+        self.sweep("A0", "C0", "F0", "V0", 3, X + 1, rows0)
+        self.halo_start(self.hV0, "yd")
         self.halo_wait(self.hE1)
         self.coefs("E1", "C1", 1, X1 + 5, 4.0)
         self.win_wait("e2", "E2")
         self.coefs("E2", "C2", 1, self.X2 + 7, 16.0)
-        self.halo_wait(self.hV0)
-        self.residual("V0", "C0", "F0", "T0", 2, X1, Y)
+        self.halo_wait(self.hV0, "y")
+        self.residual("V0", "C0", "F0", "T0", 2, X1, Y, 1, X1 - 1)
+        self.halo_wait(self.hV0, "x")
+        self.residual("V0", "C0", "F0", "T0", 2, X1, Y, 0, 1)
+        self.residual("V0", "C0", "F0", "T0", 2, X1, Y, X1 - 1, X1)
         f1 = self.squeeze(r["T0"][...])
         for c in range(C):
             for j in range(X1):
@@ -394,7 +410,6 @@
 
         self.halo_start(self.hF1)
         self.halo_wait(self.hF1)
-        self.halo_start(self.hW0)
         self.first("C1", "F1", "A1", 1, X1 + 5)
         self.sweep("A1", "C1", "F1", "B1", 2, X1 + 4)
         self.residual("B1", "C1", "F1", "T1", 3, self.X2, Y1)
@@ -403,6 +418,11 @@
         for c in range(C):
             for j in range(X1):
                 r["V1"][c, 3 + j, TOP:TOP + Y1, :] = r["B1"][c, 3 + j, TOP:TOP + Y1, :]
+            for dx in (2, X1 + 3):
+                r["V1"][c, dx, TOP - 1:TOP + Y1 + 1, :] = r["B1"][c, dx, TOP - 1:TOP + Y1 + 1, :]
+            for j in range(X1):
+                for q in (TOP - 1, TOP + Y1):
+                    r["V1"][c, 3 + j, q:q + 1, :] = r["B1"][c, 3 + j, q:q + 1, :]
         self.halo_start(self.hV1)
 
         self.win_wait("f2", "F2")
@@ -416,6 +436,8 @@
                 i = (c * self.X2 + p) * self.Y2
                 r["Sv2"][i:i + self.Y2, :] = r["B2"][c, 4 + p, self.Y2:2 * self.Y2, :]
         self.win_start("v2")
+        for h in self.hW0:
+            self.halo_start(h)
         self.win_wait("v2", "A2")
         self.sweep("A2", "C2", "F2", "B2", 1, p2 - 1)
         self.sweep("B2", "C2", "F2", "A2", 2, p2 - 2)
@@ -427,9 +449,10 @@
         self.sweep("V1", "C1", "F1", "A1", 1, X1 + 5)
         self.sweep("A1", "C1", "F1", "B1", 2, X1 + 4)
 
-        self.halo_wait(self.hW0)
+        for h in self.hW0:
+            self.halo_wait(h)
+            self.halo_sent(h)
         self.halo_sent(self.hV0)
-        self.halo_sent(self.hW0)
         self.prolong("B1", 2, X1 + 2, "UZ0", "V0", range(self.P0),
                      lambda p: 3 + (p - 2) // 2, TOP)
         self.sweep("V0", "C0", "F0", "B0", 1, X + 3)

time: 60.3 us -> 56.5 us (0.937)
  the two profiles are of different devices: /device:TPU:1 before, /device:TPU:17 now
where the time goes in v2:
time: 56.5 us; the launch traced here: 56.4 us
  Pallas kernels  54.3 us (96%)
  local copies, waits for them, and re-layouts  2.09 us (4%)
    pallas_call x1, Pallas kernels, __call__(): pl.pallas_call(self.body, out_shape=jax.ShapeDtypeStruct(forcing.shape, j...  54.3 us
    unnamed x1, local copies, waits for them, and re-layouts  2.09 us

profile of v2, /device:TPU:17, one launch (start us, length us, event | category | flops | bytes accessed | tf_op | source)
XLA Modules:
  0.0 56.4 jit_solution(7688411936195791211)
XLA Ops:
  0.0 54.3 %vcycle.1 = f32[3,8,16,512]{3,2,1,0:T(8,128)} custom-call(f32[3,8,16,512]{3,2,1,0:T(8,128)} %forcing.1, s32[8,16,512]{2,1,0:T(8,128)} %phase.1), custom_call_target="tpu_custom_call" | custom-call | tf_op jit(solution)/shard_map/vcycle/pallas_call | solution.py:472
  54.3 2.1 %copy.4 = f32[3,8,16,512]{3,2,1,0:T(8,128)} copy(f32[3,8,16,512]{3,2,1,0:T(8,128)} %vcycle.1) | data formatting | bytes 1572864

commit v3 on v2

--- a/solution.py
+++ b/solution.py
@@ -12,7 +12,7 @@
 WEIGHT = 2.0 / 3.0
 MESH = pl.DeviceIdType.MESH
 WINDOW = [(dx, dy) for dx in range(-2, 3) for dy in range(-1, 2) if (dx, dy) != (0, 0)]
-TOP = 8
+TOP = 0
 
 
 def up8(n):
@@ -49,28 +49,29 @@
         self.buf(name + "_ry", (2, up8(n), Z))
         for k, dy in enumerate((1, -1)):
             s, d = side_slices(dy, TOP, Y, lo, hi)
+            d %= Y + 8
             msgs.append(("y", k, dy, s, d, self.n_sems))
             self.n_sems += 1
         if diag:
             n = comps * len(diag)
-            self.buf(name + "_sd", (4, up8(n), Z))
-            self.buf(name + "_rd", (4, up8(n), Z))
+            self.buf(name + "_sd", (4, n, 1, Z))
+            self.buf(name + "_rd", (4, n, 1, Z))
             for k, (dx, dy) in enumerate([(1, 1), (1, -1), (-1, 1), (-1, -1)]):
                 cells = [[], []]
                 for a, b in diag:
                     sx, tx = side_slices(dx, px, X, a, a)
                     sy, ty = side_slices(dy, TOP, Y, b, b)
                     cells[0].append((sx, sy))
-                    cells[1].append((tx, ty))
+                    cells[1].append((tx, ty % (Y + 8)))
                 msgs.append(("d", k, (dx, dy), cells[0], cells[1], self.n_sems))
                 self.n_sems += 1
         return dict(name=name, base=base, target=target, comps=comps, px=px, X=X, Y=Y, w=w, diag=diag, msgs=msgs)
 
     def plan(self):
         X, Y, Z, C = self.X, self.Y, self.Z, self.C
-        self.P0, self.R0 = X + 4, Y + 16
+        self.P0, self.R0 = X + 4, Y + 8
         self.X1, self.Y1, self.Z1 = X // 2, Y // 2, Z // 2
-        self.P1, self.R1 = self.X1 + 6, self.Y1 + 16
+        self.P1, self.R1 = self.X1 + 6, self.Y1 + 8
         self.X2, self.Y2, self.Z2 = X // 4, Y // 4, Z // 4
         self.P2, self.R2 = self.X2 + 8, up8(self.Y2 * 3)
         b = self.buf
@@ -159,7 +160,11 @@
             k, kind, rows = self.rows_of(h, m, 0)
             stage = self.r[h["name"] + "_s" + kind]
             for i, (c, p, q) in enumerate(rows):
-                stage[k, i:i + 1, :] = ref[c, p, q:q + 1, :]
+                row = ref[c, p, q:q + 1, :]
+                if kind == "d":
+                    stage[k, i] = row
+                else:
+                    stage[k, i:i + 1, :] = row
         for c, dx, dy in self.halo_copies(h, kinds):
             pl.when(self.exists(dx, dy))(c.start)
 
@@ -173,7 +178,7 @@
             k, kind, rows = self.rows_of(h, m, 1)
             stage = self.r[h["name"] + "_r" + kind]
             for i, (c, p, q) in enumerate(rows):
-                ref[c, p, q:q + 1, :] = stage[k, i:i + 1, :]
+                ref[c, p, q:q + 1, :] = stage[k, i] if kind == "d" else stage[k, i:i + 1, :]
 
     def halo_sent(self, h):
         for c, dx, dy in self.halo_copies(h):
@@ -246,7 +251,7 @@
         if n == R:
             yp, ym = pltpu.roll(v, R - 1, 0), pltpu.roll(v, 1, 0)
         else:
-            yp, ym = V[c, i, rows.start + 1:rows.stop + 1, :], V[c, i, rows.start - 1:rows.stop - 1, :]
+            yp, ym = V[c, i, 1:n + 1, :], pltpu.roll(V[c, i], 1, 0)[:n]
         acc = G[c, i, rows, :]
         parts = (V[c, i + 1, rows, :], V[c, i - 1, rows, :], yp, ym, pltpu.roll(v, Z - 1, 1), pltpu.roll(v, 1, 1))
         for k, o in enumerate(parts):
@@ -289,33 +294,46 @@
                 T[pl.ds(pl.multiple_of((c * Xc + j) * Y, 8), Y), :] = 0.5 * total
 
     def dot(self, a, b):
-        return lax.dot_general(a, b, (((1,), (0,)), ((), ())), precision=lax.Precision.HIGHEST,
-                               preferred_element_type=jnp.float32)
+        return lax.dot_general(a, b, (((1,), (0,)), ((), ())), preferred_element_type=jnp.float32)
+
+    def split(self, t):
+        hi = t.astype(jnp.bfloat16)
+        return hi, (t - hi.astype(jnp.float32)).astype(jnp.bfloat16)
+
+    def right(self, t, m):
+        hi, lo = self.split(t)
+        return self.dot(hi, m) + self.dot(lo, m)
+
+    def left(self, m, t):
+        hi, lo = self.split(t)
+        return self.dot(m, hi) + self.dot(m, lo)
 
     def pairs(self, n, m, value, fine_dim):
         r = lax.broadcasted_iota(jnp.int32, (n, m), 0)
         c = lax.broadcasted_iota(jnp.int32, (n, m), 1)
         hit = (r >> 1) == c if fine_dim == 0 else (c >> 1) == r
-        return jnp.where(hit, value, 0.0).astype(jnp.float32)
+        return jnp.where(hit, value, 0.0).astype(jnp.bfloat16)
 
     def squeeze(self, t):
         rows, Z = t.shape
-        half = self.dot(t, self.pairs(Z, Z // 2, 0.5, 0))
-        return self.dot(self.pairs(rows // 2, rows, 0.5, 1), half)
+        half = self.right(t, self.pairs(Z, Z // 2, 0.5, 0))
+        return self.left(self.pairs(rows // 2, rows, 0.5, 1), half)
 
     def prolong(self, W, a, count, U, V, planes, coarse_of, offset):
         W, U, V = (self.r[n] for n in (W, U, V))
         C, _, Rc, Zc = W.shape
         Rf, Zf = V.shape[-2:]
         src = W[:, a:a + count].reshape(C * count * Rc, Zc)
-        U[...] = self.dot(src, self.pairs(Zf, Zc, 1.0, 0).T if False else self.pairs(Zc, Zf, 1.0, 1))
+        U[...] = self.right(src, self.pairs(Zc, Zf, 1.0, 1))
         r = lax.broadcasted_iota(jnp.int32, (Rf, Rc), 0)
         c = lax.broadcasted_iota(jnp.int32, (Rf, Rc), 1)
-        lift = jnp.where(((r + 2 * offset - TOP) >> 1) == c, 1.0, 0.0).astype(jnp.float32)
+        r = jnp.where(r < Rf - 4, r, r - Rf)
+        c = c - offset if offset else jnp.where(c < Rc - 4, c, c - Rc)
+        lift = jnp.where((r >> 1) == c, 1.0, 0.0).astype(jnp.bfloat16)
         for comp in range(C):
             for k in range(count):
                 start = (comp * count + k) * Rc
-                block = self.dot(lift, U[start:start + Rc, :])
+                block = self.left(lift, U[start:start + Rc, :])
                 for p in planes:
                     if coarse_of(p) == a + k:
                         V[comp, p] = V[comp, p] + block
@@ -419,9 +437,9 @@
             for j in range(X1):
                 r["V1"][c, 3 + j, TOP:TOP + Y1, :] = r["B1"][c, 3 + j, TOP:TOP + Y1, :]
             for dx in (2, X1 + 3):
-                r["V1"][c, dx, TOP - 1:TOP + Y1 + 1, :] = r["B1"][c, dx, TOP - 1:TOP + Y1 + 1, :]
-            for j in range(X1):
-                for q in (TOP - 1, TOP + Y1):
+                r["V1"][c, dx, 0:Y1, :] = r["B1"][c, dx, 0:Y1, :]
+            for j in range(-1, X1 + 1):
+                for q in (self.R1 - 1, Y1):
                     r["V1"][c, 3 + j, q:q + 1, :] = r["B1"][c, 3 + j, q:q + 1, :]
         self.halo_start(self.hV1)
 
@@ -454,7 +472,7 @@
             self.halo_sent(h)
         self.halo_sent(self.hV0)
         self.prolong("B1", 2, X1 + 2, "UZ0", "V0", range(self.P0),
-                     lambda p: 3 + (p - 2) // 2, TOP)
+                     lambda p: 3 + (p - 2) // 2, 0)
         self.sweep("V0", "C0", "F0", "B0", 1, X + 3)
         self.sweep("B0", "C0", "F0", "O0", 2, X + 2, rows0, shift=2)
         store = pltpu.make_async_copy(r["O0"], out, lsem.at[0])

time: 56.5 us -> 49.8 us (0.88)
  Pallas kernels: 54.3 us -> 47.5 us
    pallas_call x1, Pallas kernels: 54.3 us -> 47.5 us  [__call__(): pl.pallas_call(self.body, out_shape=jax.ShapeDtypeStruct(forcing.shape, j...]
where the time goes in v3:
time: 49.8 us; the launch traced here: 49.6 us
  Pallas kernels  47.5 us (95%)
  local copies, waits for them, and re-layouts  2.09 us (4%)
    pallas_call x1, Pallas kernels, __call__(): pl.pallas_call(self.body, out_shape=jax.ShapeDtypeStruct(forcing.shape, j...  47.5 us
    unnamed x1, local copies, waits for them, and re-layouts  2.09 us

profile of v3, /device:TPU:17, one launch (start us, length us, event | category | flops | bytes accessed | tf_op | source)
XLA Modules:
  0.0 49.6 jit_solution(16571871794873129763)
XLA Ops:
  0.0 47.5 %vcycle.1 = f32[3,8,16,512]{3,2,1,0:T(8,128)} custom-call(f32[3,8,16,512]{3,2,1,0:T(8,128)} %forcing.1, s32[8,16,512]{2,1,0:T(8,128)} %phase.1), custom_call_target="tpu_custom_call" | custom-call | tf_op jit(solution)/shard_map/vcycle/pallas_call | solution.py:490
  47.5 2.1 %copy.4 = f32[3,8,16,512]{3,2,1,0:T(8,128)} copy(f32[3,8,16,512]{3,2,1,0:T(8,128)} %vcycle.1) | data formatting | bytes 1572864

commit v4 on v3

--- a/solution.py
+++ b/solution.py
@@ -99,8 +99,8 @@
         b("UZ0", (self.R1 * C * (self.X1 + 2), self.Z))
         reach = [(1, 1), (1, 2), (2, 1), (1, 3), (2, 2), (3, 1)]
         self.hE0 = self.halo("hE0", "E0", 1, 2, X, Y, Z, 1, 2, [(1, 1)])
-        self.hF0 = self.halo("hF0", "F0", C, 2, X, Y, Z, 1, 1, [])
-        self.hV0 = self.halo("hV0", "V0", C, 2, X, Y, Z, 1, 1, [])
+        self.hF0 = [self.halo("hFc%d" % c, "F0", 1, 2, X, Y, Z, 1, 1, [], c) for c in range(C)]
+        self.hV0 = [self.halo("hVc%d" % c, "V0", 1, 2, X, Y, Z, 1, 1, [], c) for c in range(C)]
         self.hW0 = [self.halo("hW%d" % c, "V0", 1, 2, X, Y, Z, 2, 2, [(1, 1)], c) for c in range(C)]
         self.hE1 = self.halo("hE1", "E1", 1, 3, self.X1, self.Y1, self.Z1, 1, 3, reach)
         self.hF1 = self.halo("hF1", "F1", C, 3, self.X1, self.Y1, self.Z1, 1, 2, reach[:3])
@@ -258,33 +258,33 @@
             acc = acc + K[k, i, rows, :] * o
         return v, acc
 
-    def first(self, K, G, O, a, b):
+    def first(self, K, G, O, a, b, comps=None):
         K, G, O = (self.r[n] for n in (K, G, O))
 
         @pl.loop(a, b)
         def _(i):
             w = K[6, i]
-            for c in range(self.C):
+            for c in comps or range(self.C):
                 O[c, i] = w * G[c, i]
 
-    def sweep(self, V, K, G, O, a, b, rows=None, shift=0):
+    def sweep(self, V, K, G, O, a, b, rows=None, shift=0, comps=None):
         V, K, G, O = (self.r[n] for n in (V, K, G, O))
         rows = rows or slice(0, V.shape[-2])
         out_rows = rows if shift == 0 else slice(0, rows.stop - rows.start)
 
         @pl.loop(a, b)
         def _(i):
-            for c in range(self.C):
+            for c in comps or range(self.C):
                 v, acc = self.stencil(V, K, G, i, c, rows)
                 O[c, i - shift, out_rows, :] = (1.0 - WEIGHT) * v + K[6, i, rows, :] * acc
 
-    def residual(self, V, K, G, T, px, Xc, Y, a=0, b=None):
+    def residual(self, V, K, G, T, px, Xc, Y, a=0, b=None, comps=None):
         V, K, G, T = (self.r[n] for n in (V, K, G, T))
         rows = slice(TOP, TOP + Y)
 
         @pl.loop(a, Xc if b is None else b)
         def _(j):
-            for c in range(self.C):
+            for c in comps or range(self.C):
                 total = None
                 for q in range(2):
                     i = px + 2 * j + q
@@ -383,7 +383,8 @@
         pl.semaphore_wait(barrier, count)
         self.halo_start(self.hE0)
         load_f.wait()
-        self.halo_start(self.hF0)
+        for h in self.hF0:
+            self.halo_start(h)
 
         for j in range(X1):
             r["T0"][j * Y:(j + 1) * Y, :] = 0.5 * (
@@ -391,35 +392,35 @@
         e1 = self.squeeze(r["T0"][0:X1 * Y, :])
         for j in range(X1):
             r["E1"][0, 3 + j, TOP:TOP + Y1, :] = e1[j * Y1:(j + 1) * Y1]
-        self.halo_start(self.hE1)
         for j in range(self.X2):
             r["T1"][j * Y1:(j + 1) * Y1, :] = 0.5 * (
                 e1[2 * j * Y1:(2 * j + 1) * Y1] + e1[(2 * j + 1) * Y1:(2 * j + 2) * Y1])
         r["Se2"][...] = self.squeeze(r["T1"][0:self.X2 * Y1, :])
-        self.win_start("e2")
 
         self.halo_wait(self.hE0, "y")
         self.coefs("E0", "C0", 3, X + 1, 1.0)
         self.halo_wait(self.hE0, "xd")
         self.coefs("E0", "C0", 1, 3, 1.0)
         self.coefs("E0", "C0", X + 1, X + 3, 1.0)
-        self.halo_wait(self.hF0)
-        self.first("C0", "F0", "A0", 1, X + 3)
         rows0 = slice(TOP, TOP + Y)
-        self.sweep("A0", "C0", "F0", "V0", 2, 3, rows0)
-        self.sweep("A0", "C0", "F0", "V0", X + 1, X + 2, rows0)
-        self.halo_start(self.hV0, "x")
+        for c in range(C):
+            self.halo_wait(self.hF0[c])
+            self.first("C0", "F0", "A0", 1, X + 3, [c])
+            self.sweep("A0", "C0", "F0", "V0", 2, 3, rows0, comps=[c])
+            self.sweep("A0", "C0", "F0", "V0", X + 1, X + 2, rows0, comps=[c])
+            self.halo_start(self.hV0[c], "x")
         self.sweep("A0", "C0", "F0", "V0", 3, X + 1, rows0)
-        self.halo_start(self.hV0, "yd")
-        self.halo_wait(self.hE1)
-        self.coefs("E1", "C1", 1, X1 + 5, 4.0)
-        self.win_wait("e2", "E2")
-        self.coefs("E2", "C2", 1, self.X2 + 7, 16.0)
-        self.halo_wait(self.hV0, "y")
+        for h in self.hV0:
+            self.halo_start(h, "y")
+        self.halo_start(self.hE1)
+        self.win_start("e2")
+        for h in self.hV0:
+            self.halo_wait(h, "y")
         self.residual("V0", "C0", "F0", "T0", 2, X1, Y, 1, X1 - 1)
-        self.halo_wait(self.hV0, "x")
-        self.residual("V0", "C0", "F0", "T0", 2, X1, Y, 0, 1)
-        self.residual("V0", "C0", "F0", "T0", 2, X1, Y, X1 - 1, X1)
+        for c in range(C):
+            self.halo_wait(self.hV0[c], "x")
+            self.residual("V0", "C0", "F0", "T0", 2, X1, Y, 0, 1, [c])
+            self.residual("V0", "C0", "F0", "T0", 2, X1, Y, X1 - 1, X1, [c])
         f1 = self.squeeze(r["T0"][...])
         for c in range(C):
             for j in range(X1):
@@ -427,6 +428,8 @@
                 r["F1"][c, 3 + j, TOP:TOP + Y1, :] = f1[s:s + Y1]
 
         self.halo_start(self.hF1)
+        self.halo_wait(self.hE1)
+        self.coefs("E1", "C1", 1, X1 + 5, 4.0)
         self.halo_wait(self.hF1)
         self.first("C1", "F1", "A1", 1, X1 + 5)
         self.sweep("A1", "C1", "F1", "B1", 2, X1 + 4)
@@ -443,6 +446,8 @@
                     r["V1"][c, 3 + j, q:q + 1, :] = r["B1"][c, 3 + j, q:q + 1, :]
         self.halo_start(self.hV1)
 
+        self.win_wait("e2", "E2")
+        self.coefs("E2", "C2", 1, self.X2 + 7, 16.0)
         self.win_wait("f2", "F2")
         p2 = self.P2
         self.first("C2", "F2", "A2", 1, p2 - 1)
@@ -470,14 +475,15 @@
         for h in self.hW0:
             self.halo_wait(h)
             self.halo_sent(h)
-        self.halo_sent(self.hV0)
+        for h in self.hV0:
+            self.halo_sent(h)
         self.prolong("B1", 2, X1 + 2, "UZ0", "V0", range(self.P0),
                      lambda p: 3 + (p - 2) // 2, 0)
         self.sweep("V0", "C0", "F0", "B0", 1, X + 3)
         self.sweep("B0", "C0", "F0", "O0", 2, X + 2, rows0, shift=2)
         store = pltpu.make_async_copy(r["O0"], out, lsem.at[0])
         store.start()
-        for h in (self.hE0, self.hF0, self.hE1, self.hF1):
+        for h in (self.hE0, *self.hF0, self.hE1, self.hF1):
             self.halo_sent(h)
         for n in ("e2", "f2", "v2"):
             self.win_sent(n)

time: 49.8 us -> 48.9 us (0.982)
  Pallas kernels: 47.5 us -> 46.2 us
    pallas_call x1, Pallas kernels: 47.5 us -> 46.2 us  [__call__(): pl.pallas_call(self.body, out_shape=jax.ShapeDtypeStruct(forcing.shape, j...]
where the time goes in v4:
time: 48.9 us; the launch traced here: 48.3 us
  Pallas kernels  46.2 us (94%)
  local copies, waits for them, and re-layouts  2.09 us (4%)
    pallas_call x1, Pallas kernels, __call__(): pl.pallas_call(self.body, out_shape=jax.ShapeDtypeStruct(forcing.shape, j...  46.2 us
    unnamed x1, local copies, waits for them, and re-layouts  2.09 us

profile of v4, /device:TPU:17, one launch (start us, length us, event | category | flops | bytes accessed | tf_op | source)
XLA Modules:
  0.0 48.3 jit_solution(15965000707666435922)
XLA Ops:
  0.0 46.2 %vcycle.1 = f32[3,8,16,512]{3,2,1,0:T(8,128)} custom-call(f32[3,8,16,512]{3,2,1,0:T(8,128)} %forcing.1, s32[8,16,512]{2,1,0:T(8,128)} %phase.1), custom_call_target="tpu_custom_call" | custom-call | tf_op jit(solution)/shard_map/vcycle/pallas_call | solution.py:496
  46.2 2.1 %copy.4 = f32[3,8,16,512]{3,2,1,0:T(8,128)} copy(f32[3,8,16,512]{3,2,1,0:T(8,128)} %vcycle.1) | data formatting | bytes 1572864

commit v5 on v4

--- a/solution.py
+++ b/solution.py
@@ -348,7 +348,16 @@
         block = (pl.ds(2, X), pl.ds(TOP, Y))
         load_p = pltpu.make_async_copy(phase, r["ph"], lsem.at[0])
         load_p.start()
-        for n in ("E0", "F0", "V0", "E1", "F1", "V1", "E2", "F2", "A2"):
+        for n in ("F0", "V0"):
+            ref = r[n]
+            for c in range(C):
+                for p in (0, 1, X + 2, X + 3):
+                    ref[c, p, 0:Y, :] = jnp.zeros((Y, Z), jnp.float32)
+
+                @pl.loop(0, self.P0)
+                def _(i):
+                    ref[c, i, Y:self.R0, :] = jnp.zeros((self.R0 - Y, Z), jnp.float32)
+        for n in ("E0", "E1", "F1", "V1", "E2", "F2", "A2"):
             ref = r[n]
             for c in range(ref.shape[0]):
                 @pl.loop(0, ref.shape[1])
@@ -445,6 +454,7 @@
                 for q in (self.R1 - 1, Y1):
                     r["V1"][c, 3 + j, q:q + 1, :] = r["B1"][c, 3 + j, q:q + 1, :]
         self.halo_start(self.hV1)
+        self.halo_start(self.hW0[0])
 
         self.win_wait("e2", "E2")
         self.coefs("E2", "C2", 1, self.X2 + 7, 16.0)
@@ -459,7 +469,7 @@
                 i = (c * self.X2 + p) * self.Y2
                 r["Sv2"][i:i + self.Y2, :] = r["B2"][c, 4 + p, self.Y2:2 * self.Y2, :]
         self.win_start("v2")
-        for h in self.hW0:
+        for h in self.hW0[1:]:
             self.halo_start(h)
         self.win_wait("v2", "A2")
         self.sweep("A2", "C2", "F2", "B2", 1, p2 - 1)

time: 48.9 us -> 48.3 us (0.988)
  Pallas kernels: 46.2 us -> 45.7 us
    pallas_call x1, Pallas kernels: 46.2 us -> 45.7 us  [__call__(): pl.pallas_call(self.body, out_shape=jax.ShapeDtypeStruct(forcing.shape, j...]
where the time goes in v5:
time: 48.3 us; the launch traced here: 47.8 us
  Pallas kernels  45.7 us (95%)
  local copies, waits for them, and re-layouts  2.09 us (4%)
    pallas_call x1, Pallas kernels, __call__(): pl.pallas_call(self.body, out_shape=jax.ShapeDtypeStruct(forcing.shape, j...  45.7 us
    unnamed x1, local copies, waits for them, and re-layouts  2.09 us

profile of v5, /device:TPU:17, one launch (start us, length us, event | category | flops | bytes accessed | tf_op | source)
XLA Modules:
  0.0 47.8 jit_solution(8839876159815670104)
XLA Ops:
  0.0 45.7 %vcycle.1 = f32[3,8,16,512]{3,2,1,0:T(8,128)} custom-call(f32[3,8,16,512]{3,2,1,0:T(8,128)} %forcing.1, s32[8,16,512]{2,1,0:T(8,128)} %phase.1), custom_call_target="tpu_custom_call" | custom-call | tf_op jit(solution)/shard_map/vcycle/pallas_call | solution.py:506
  45.7 2.1 %copy.4 = f32[3,8,16,512]{3,2,1,0:T(8,128)} copy(f32[3,8,16,512]{3,2,1,0:T(8,128)} %vcycle.1) | data formatting | bytes 1572864
